TPU v7x, 128 devices: a whole 4x4x4 slice. The times are simulated.
128 devices in a mesh: dp: 32 (over x, z, core), mp: 4 (over y).
Axes of the slice: x: 4, y: 4, z: 4, core: 2. Of those that a mesh axis runs over, the one named last changes fastest.
Arguments:
- tokens: bfloat16 [8192, 1024], P('dp', 'mp'), may hold values from -6 to 6
- grad_out: bfloat16 [8192, 1024], P('dp', 'mp'), may hold values from -6 to 6
- gates: bfloat16 [8192, 2], P('dp'), may hold values from 0.099609375 to 0.8984375
- expert_ids: int32 [8192, 2], P('dp'), may hold values from 0 to 63, all different within a row; in each aligned block of 256 rows (0 to 255, 256 to 511, ...) at most 16 rows name the same one
- w_gate: bfloat16 [64, 1024, 4096], P('dp', None, 'mp'), may hold values from -0.1875 to 0.1875
- w_up: bfloat16 [64, 1024, 4096], P('dp', None, 'mp'), may hold values from -0.1875 to 0.1875
- w_down: bfloat16 [64, 4096, 1024], P('dp', 'mp'), may hold values from -0.09375 to 0.09375
Outputs:
- grad_tokens: bfloat16 [8192, 1024], P('dp', 'mp')
- grad_gates: float32 [8192, 2], P('dp')
- grad_w_gate: bfloat16 [64, 1024, 4096], P('dp', None, 'mp')
- grad_w_up: bfloat16 [64, 1024, 4096], P('dp', None, 'mp')
- grad_w_down: bfloat16 [64, 4096, 1024], P('dp', 'mp')
Inputs may be any that keep to these rules, and one draw needn't show every extreme that they name: `expert_ids`: among the 256 tokens of one index of dp no expert is named more than 16 times, and in some such block some expert is named exactly 16 times; the two experts of a token differ.
All inputs are finite; a program needn't handle non-finite values.
Results may differ from a plain program's by a relative error of at most 0.0058.
Values may be sent and summed in bfloat16 or wider, within the bound.
A program may use at most 128 MiB of HBM per device.

v0:
```python
import jax
import jax.numpy as jnp
from jax import lax
from jax.sharding import PartitionSpec as P


def on_device(tokens, grad_out, gates, expert_ids, w_gate, w_up, w_down):
    count_tokens = tokens.shape[0]
    width_share = tokens.shape[1]
    groups = lax.axis_size("dp")
    local_experts = w_gate.shape[0]
    width_full = w_down.shape[2]
    all_experts = local_experts * groups
    capacity = max(2, 4 * count_tokens // all_experts)
    total_slots = all_experts * capacity
    onehot = (
        expert_ids[:, :, None] == jnp.arange(all_experts, dtype=jnp.int32)[None, None, :]
    ).astype(jnp.int32)
    onehot = onehot.reshape(count_tokens * 2, all_experts)
    before = jnp.cumsum(onehot, axis=0) - onehot
    position = jnp.sum(before * onehot, axis=1)
    slot_of = expert_ids.reshape(-1) * capacity + position
    placed = slot_of[None, :] == jnp.arange(total_slots, dtype=jnp.int32)[:, None]
    placed = placed.astype(jnp.bfloat16).reshape(total_slots, count_tokens, 2)
    route = jnp.sum(placed.astype(jnp.float32), axis=2).astype(jnp.bfloat16)
    slot_gate = jnp.einsum("stk,tk->s", placed, gates, preferred_element_type=jnp.float32).astype(
        jnp.bfloat16
    )
    slot_gate = slot_gate.reshape(groups, local_experts * capacity)
    full_x, full_dy = (
        lax.all_gather(tokens, "mp", axis=1, tiled=True),
        lax.all_gather(grad_out, "mp", axis=1, tiled=True),
    )
    send_x = jnp.dot(route, full_x, preferred_element_type=jnp.float32).astype(jnp.bfloat16)
    send_dy = jnp.dot(route, full_dy, preferred_element_type=jnp.float32).astype(jnp.bfloat16)
    send_x = send_x.reshape(groups, local_experts * capacity, width_full)
    send_dy = send_dy.reshape(groups, local_experts * capacity, width_full)
    recv_x, recv_dy, recv_gate = (
        lax.all_to_all(send_x, "dp", split_axis=0, concat_axis=0, tiled=True),
        lax.all_to_all(send_dy, "dp", split_axis=0, concat_axis=0, tiled=True),
        lax.all_to_all(slot_gate, "dp", split_axis=0, concat_axis=0, tiled=True),
    )
    recv_x = recv_x.reshape(groups, local_experts, capacity, width_full)
    recv_dy = recv_dy.reshape(groups, local_experts, capacity, width_full)
    recv_gate = recv_gate.reshape(groups, local_experts, capacity)
    grads_gate = []
    grads_up = []
    grads_down = []
    input_parts = []
    gate_parts = []
    for expert in range(local_experts):
        rows_x = recv_x[:, expert]
        rows_dy = recv_dy[:, expert]
        rows_gate = recv_gate[:, expert]
        gate_pre = jnp.einsum(
            "scd,df->scf", rows_x, w_gate[expert], preferred_element_type=jnp.float32
        )
        up_pre = jnp.einsum("scd,df->scf", rows_x, w_up[expert], preferred_element_type=jnp.float32)
        sigmoid_gate = jax.nn.sigmoid(gate_pre)
        activated = gate_pre * sigmoid_gate
        hidden = (activated * up_pre).astype(jnp.bfloat16)
        output_part = jnp.einsum(
            "scf,fd->scd", hidden, w_down[expert], preferred_element_type=jnp.float32
        )
        gate_parts.append(jnp.sum(rows_dy.astype(jnp.float32) * output_part, axis=2))
        scaled = (rows_gate.astype(jnp.float32)[:, :, None] * rows_dy.astype(jnp.float32)).astype(
            jnp.bfloat16
        )
        hidden_grad = jnp.einsum(
            "scd,fd->scf", scaled, w_down[expert], preferred_element_type=jnp.float32
        )
        dgate = (
            hidden_grad * up_pre * sigmoid_gate * (1.0 + gate_pre * (1.0 - sigmoid_gate))
        ).astype(jnp.bfloat16)
        dup = (hidden_grad * activated).astype(jnp.bfloat16)
        grads_down.append(
            jnp.einsum("scf,scd->fd", hidden, scaled, preferred_element_type=jnp.float32).astype(
                jnp.bfloat16
            )
        )
        grads_gate.append(
            jnp.einsum("scd,scf->df", rows_x, dgate, preferred_element_type=jnp.float32).astype(
                jnp.bfloat16
            )
        )
        grads_up.append(
            jnp.einsum("scd,scf->df", rows_x, dup, preferred_element_type=jnp.float32).astype(
                jnp.bfloat16
            )
        )
        input_parts.append(
            jnp.einsum("scf,df->scd", dgate, w_gate[expert], preferred_element_type=jnp.float32)
            + jnp.einsum("scf,df->scd", dup, w_up[expert], preferred_element_type=jnp.float32)
        )
    gate_stack = jnp.stack(gate_parts, axis=1)
    input_stack = jnp.stack(input_parts, axis=1)
    gate_total = lax.psum(gate_stack, "mp")
    back_gates = lax.all_to_all(gate_total, "dp", split_axis=0, concat_axis=0, tiled=True)
    back_gates = back_gates.reshape(total_slots)
    grad_gates = jnp.take(back_gates, slot_of, axis=0).reshape(count_tokens, 2)
    input_share = lax.psum_scatter(input_stack, "mp", scatter_dimension=3, tiled=True)
    back_rows = lax.all_to_all(input_share, "dp", split_axis=0, concat_axis=0, tiled=True)
    back_rows = back_rows.reshape(total_slots, width_share)
    picked = jnp.take(back_rows, slot_of, axis=0).reshape(count_tokens, 2, width_share)
    grad_tokens = jnp.sum(picked, axis=1).astype(jnp.bfloat16)
    return (
        grad_tokens,
        grad_gates,
        jnp.stack(grads_gate, axis=0),
        jnp.stack(grads_up, axis=0),
        jnp.stack(grads_down, axis=0),
    )


def solution(mesh):
    placed = (
        P("dp", "mp"),
        P("dp", "mp"),
        P("dp", None),
        P("dp", None),
        P("dp", None, "mp"),
        P("dp", None, "mp"),
        P("dp", "mp", None),
    )
    return jax.shard_map(
        on_device,
        mesh=mesh,
        in_specs=placed,
        out_specs=(
            P("dp", "mp"),
            P("dp", None),
            P("dp", None, "mp"),
            P("dp", None, "mp"),
            P("dp", "mp", None),
        ),
        check_vma=False,
    )
```

profile of v0, /device:TPU:1, one launch (start us, length us, event | category | flops | bytes accessed | tf_op | source)
XLA Modules:
  0.0 213.9 jit_solution(18338866497481159757)
XLA Ops:
  11.4 9.4 %all-to-all-start = ((bf16[32,1,32]{2,1,0:T(2,128)(2,1)}), bf16[32,1,32]{2,1,0:T(2,128)(2,1)S(1)}, u32[]{:S(2)}, u32[]{:S(2)}) async-start(bf16[32,1,32]{2,1,0:T(2,128)(2,1)} %all_to_all.24), calls=%async_computation | async-start | bytes 32768 | tf_op jit(solution)/shard_map/all_to_all | solution.py:41
  21.3 11.1 %all_gather.7 = bf16[256,1024]{1,0:T(8,128)(2,1)S(1)} all-gather(bf16[256,256]{1,0:T(8,128)(2,1)S(1)} %copy-done.9), channel_id=1, replica_groups=mesh['dp'=32,'mp'=4] {'mp'}, dimensions={1}, use_global_device_ids=true | all-gather | bytes 655360 | tf_op jit(solution)/shard_map/all_gather | solution.py:31
  34.5 9.7 %all-to-all-start.2 = ((bf16[32,32,1024]{2,1,0:T(8,128)(2,1)}), bf16[32,32,1024]{2,1,0:T(8,128)(2,1)S(1)}, u32[]{:S(2)}, u32[]{:S(2)}) async-start(bf16[32,32,1024]{2,1,0:T(8,128)(2,1)} %bitcast.10), calls=%async_computation.2 | async-start | bytes 4194304 | tf_op jit(solution)/shard_map/all_to_all | solution.py:39
  44.2 11.5 %all_gather.6 = bf16[256,1024]{1,0:T(8,128)(2,1)S(1)} all-gather(bf16[256,256]{1,0:T(8,128)(2,1)S(1)} %copy-done.10), channel_id=1, replica_groups=mesh['dp'=32,'mp'=4] {'mp'}, dimensions={1}, use_global_device_ids=true | all-gather | bytes 655360 | tf_op jit(solution)/shard_map/all_gather | solution.py:32
  55.7 2.0 convolution_convert_fusion.1
  57.8 14.8 %all-to-all-done.2 = bf16[32,32,1024]{2,1,0:T(8,128)(2,1)S(1)} async-done(((bf16[32,32,1024]{2,1,0:T(8,128)(2,1)}), bf16[32,32,1024]{2,1,0:T(8,128)(2,1)S(1)}, u32[]{:S(2)}, u32[]{:S(2)}) %all-to-all-start.2) | async-done | bytes 2097184 | tf_op jit(solution)/shard_map/all_to_all | solution.py:39
  72.5 5.2 %all-to-all-start.1 = ((bf16[32,32,1024]{2,1,0:T(8,128)(2,1)}), bf16[32,32,1024]{2,1,0:T(8,128)(2,1)}, u32[]{:S(2)}, u32[]{:S(2)}) async-start(bf16[32,32,1024]{2,1,0:T(8,128)(2,1)} %bitcast.5), calls=%async_computation.1 | async-start | bytes 4194304 | tf_op jit(solution)/shard_map/all_to_all | solution.py:40
  78.9 4.3 %fusion.12 = f32[32,16,1024]{2,1,0:T(8,128)} fusion(bf16[2,1024,1024]{2,1,0:T(8,128)(2,1)} %param.11, bf16[32,2,16,1024]{3,2,1,0:T(8,128)(2,1)S(1)} %bitcast.215), kind=kOutput, calls=%fused_computation.28 | convolution fusion | flops 1073741824 | bytes 5242880 | tf_op jit(solution)/shard_map/scd,df->scf/dot_general | solution.py:55
  83.3 2.6 %fusion.24 = f32[32,16,1024]{2,1,0:T(8,128)} fusion(bf16[2,1024,1024]{2,1,0:T(8,128)(2,1)S(1)} %copy-done.12, bf16[32,2,16,1024]{3,2,1,0:T(8,128)(2,1)S(1)} %bitcast.216), kind=kOutput, calls=%fused_computation.40 | convolution fusion | flops 1073741824 | bytes 5242880 | tf_op jit(solution)/shard_map/scd,df->scf/dot_general | solution.py:55
  85.8 20.3 %all-to-all-done.1 = bf16[32,32,1024]{2,1,0:T(8,128)(2,1)} async-done(((bf16[32,32,1024]{2,1,0:T(8,128)(2,1)}), bf16[32,32,1024]{2,1,0:T(8,128)(2,1)}, u32[]{:S(2)}, u32[]{:S(2)}) %all-to-all-start.1) | async-done | bytes 2097184 | tf_op jit(solution)/shard_map/all_to_all | solution.py:40
  106.2 3.4 %fusion.20 = f32[32,16,1024]{2,1,0:T(8,128)S(1)} fusion(bf16[2,1024,1024]{2,1,0:T(8,128)(2,1)} %param.13, f32[32,16]{1,0:T(8,128)S(1)} %copy.79, bf16[32,2,16,1024]{3,2,1,0:T(8,128)(2,1)} %bitcast.6), kind=kOutput, calls=%fused_computation.36 | convolution fusion | flops 1075314688 | bytes 5244928 | tf_op jit(solution)/shard_map/scd,fd->scf/dot_general | solution.py:69
  110.0 3.0 %multiply_convert_fusion = (bf16[32,16,1024]{2,1,0:T(8,128)(2,1)}, bf16[32,16,1024]{2,1,0:T(8,128)(2,1)S(1)}, bf16[32,16,1024]{2,1,0:T(8,128)(2,1)S(1)}) fusion(f32[32,16,1024]{2,1,0:T(8,128)S(1)} %copy-done.19, f32[32,16,1024]{2,1,0:T(8,128)S(1)} %fusion.20, bf16[2,1024,1024]{2,1,0:T(8,128)(2,1)S(1)} %copy-done.14, bf16[32,2,16,1024]{3,2,1,0:T(8,128)(2,1)S(1)} %bitcast.217), kind=kOutput, calls=%fused_computation.50 | convolution fusion | flops 1081606144 | bytes 10485760 | tf_op jit(solution)/shard_map/scd,df->scf/dot_general | solution.py:58
  116.2 2.7 %fusion.32 = f32[32,16,1024]{2,1,0:T(8,128)S(1)} fusion(bf16[2,1024,1024]{2,1,0:T(8,128)(2,1)S(1)} %copy-done.15, f32[32,16]{1,0:T(8,128)S(1)} %copy.76, bf16[32,2,16,1024]{3,2,1,0:T(8,128)(2,1)} %bitcast.6), kind=kOutput, calls=%fused_computation.48 | convolution fusion | flops 1075314688 | bytes 5259264 | tf_op jit(solution)/shard_map/scd,fd->scf/dot_general | solution.py:69
  118.9 3.0 %multiply_convert_fusion.1 = (bf16[32,16,1024]{2,1,0:T(8,128)(2,1)}, bf16[32,16,1024]{2,1,0:T(8,128)(2,1)S(1)}, bf16[32,16,1024]{2,1,0:T(8,128)(2,1)S(1)}) fusion(f32[32,16,1024]{2,1,0:T(8,128)S(1)} %copy-done.18, f32[32,16,1024]{2,1,0:T(8,128)S(1)} %fusion.32, bf16[2,1024,1024]{2,1,0:T(8,128)(2,1)S(1)} %copy-done.14, ...), kind=kOutput, calls=%fused_computation.51 | convolution fusion | flops 1081606144 | bytes 10485760 | tf_op jit(solution)/shard_map/scd,df->scf/dot_general | solution.py:58
  126.0 2.5 %pad_maximum_fusion = f32[32,2,16,1024]{3,2,0,1:T(8,128)} fusion(f32[32,1,16,1024]{3,2,0,1:T(8,128)S(1)} %add_bitcast_fusion, f32[32,1,16,1024]{3,2,0,1:T(8,128)S(1)} %add_bitcast_fusion.1), kind=kLoop, calls=%fused_computation.2 | loop fusion | flops 1048576 | bytes 8388608 | tf_op jit(solution)/shard_map/stack | solution.py:96
  128.6 3.7 %fusion.7 = f32[32,16]{1,0:T(8,128)S(1)} fusion(bf16[32,16,1024]{2,1,0:T(8,128)(2,1)} %get-tuple-element.25, bf16[2,1024,1024]{2,1,0:T(8,128)(2,1)} %param.13, bf16[32,2,16,1024]{3,2,1,0:T(8,128)(2,1)} %bitcast.6), kind=kOutput, calls=%fused_computation.23 | convolution fusion | flops 1075314176 | bytes 4196352 | tf_op jit(solution)/shard_map/scf,fd->scd/dot_general | solution.py:62
  132.3 2.6 %fusion.4 = f32[32,16]{1,0:T(8,128)S(1)} fusion(bf16[32,16,1024]{2,1,0:T(8,128)(2,1)S(1)} %copy-done.24, bf16[2,1024,1024]{2,1,0:T(8,128)(2,1)S(1)} %copy-done.16, bf16[32,2,16,1024]{3,2,1,0:T(8,128)(2,1)} %bitcast.6), kind=kOutput, calls=%fused_computation.20 | convolution fusion | flops 1075314176 | bytes 4196352 | tf_op jit(solution)/shard_map/scf,fd->scd/dot_general | solution.py:62
  135.0 17.0 %psum.7 = f32[32,2,16]{2,1,0:T(2,128)} all-reduce(f32[32,2,16]{2,1,0:T(2,128)S(1)} %pad_maximum_fusion.4), channel_id=1, replica_groups=mesh['dp'=32,'mp'=4] {'mp'}, use_global_device_ids=true, to_apply=%region_8.9 | all-reduce | flops 1024 | bytes 8192 | tf_op jit(solution)/shard_map/psum | solution.py:97
  151.9 7.1 %all-to-all-start.4 = ((f32[32,2,16]{2,1,0:T(2,128)}), f32[32,2,16]{2,1,0:T(2,128)}, u32[]{:S(2)}, u32[]{:S(2)}) async-start(f32[32,2,16]{2,1,0:T(2,128)} %psum.7), calls=%async_computation.5 | async-start | bytes 65536 | tf_op jit(solution)/shard_map/all_to_all | solution.py:98
  159.0 4.0 %fusion.51 = bf16[1,1024,1024]{2,1,0:T(8,128)(2,1)} fusion(bf16[32,16,1024]{2,1,0:T(8,128)(2,1)} %copy-done.20, bf16[32,2,16,1024]{3,2,1,0:T(8,128)(2,1)S(1)} %bitcast.219), kind=kOutput, calls=%fused_computation.80 | convolution fusion | flops 1074790400 | bytes 4194304 | tf_op jit(solution)/shard_map/scd,scf->df/dot_general | solution.py:82
  163.0 2.6 %fusion.50 = bf16[1,1024,1024]{2,1,0:T(8,128)(2,1)} fusion(bf16[32,16,1024]{2,1,0:T(8,128)(2,1)S(1)} %copy-done.22, bf16[32,2,16,1024]{3,2,1,0:T(8,128)(2,1)S(1)} %bitcast.220), kind=kOutput, calls=%fused_computation.79 | convolution fusion | flops 1074790400 | bytes 4194304 | tf_op jit(solution)/shard_map/scd,scf->df/dot_general | solution.py:82
  165.7 4.0 %fusion.55 = bf16[1,1024,1024]{2,1,0:T(8,128)(2,1)} fusion(bf16[32,16,1024]{2,1,0:T(8,128)(2,1)S(1)} %copy-done.23, f32[32,16]{1,0:T(8,128)S(1)} %copy.79, bf16[32,2,16,1024]{3,2,1,0:T(8,128)(2,1)} %bitcast.6), kind=kOutput, calls=%fused_computation.84 | convolution fusion | flops 1076363264 | bytes 4196352 | tf_op jit(solution)/shard_map/scf,scd->fd/dot_general | solution.py:77
  169.7 3.9 %fusion.54 = bf16[1,1024,1024]{2,1,0:T(8,128)(2,1)} fusion(bf16[32,16,1024]{2,1,0:T(8,128)(2,1)S(1)} %copy-done.25, f32[32,16]{1,0:T(8,128)S(1)} %copy.76, bf16[32,2,16,1024]{3,2,1,0:T(8,128)(2,1)} %bitcast.6), kind=kOutput, calls=%fused_computation.83 | convolution fusion | flops 1076363264 | bytes 4196352 | tf_op jit(solution)/shard_map/scf,scd->fd/dot_general | solution.py:77
  173.6 2.6 %fusion.53 = bf16[1,1024,1024]{2,1,0:T(8,128)(2,1)} fusion(bf16[32,16,1024]{2,1,0:T(8,128)(2,1)S(1)} %get-tuple-element.27, bf16[32,2,16,1024]{3,2,1,0:T(8,128)(2,1)S(1)} %bitcast.221), kind=kOutput, calls=%fused_computation.82 | convolution fusion | flops 1074790400 | bytes 4194304 | tf_op jit(solution)/shard_map/scd,scf->df/dot_general | solution.py:87
  176.2 2.4 %copy.82 = f32[32,2,16,256]{3,2,1,0:T(8,128)} copy(f32[32,2,16,256]{3,2,0,1:T(8,128)} %reduce-scatter.2.cloned.1.call-done) | data formatting | bytes 2097152 | tf_op jit(solution)/shard_map/reduce_scatter | solution.py:101
  178.6 7.5 %all-to-all-start.3 = ((f32[32,2,16,256]{3,2,1,0:T(8,128)}), f32[32,2,16,256]{3,2,1,0:T(8,128)S(1)}, u32[]{:S(2)}, u32[]{:S(2)}) async-start(f32[32,2,16,256]{3,2,1,0:T(8,128)} %copy.82), calls=%async_computation.4 | async-start | bytes 2097152 | tf_op jit(solution)/shard_map/all_to_all | solution.py:102
  186.1 2.7 %fusion.52 = bf16[1,1024,1024]{2,1,0:T(8,128)(2,1)S(1)} fusion(bf16[32,16,1024]{2,1,0:T(8,128)(2,1)} %copy-done.17, bf16[32,2,16,1024]{3,2,1,0:T(8,128)(2,1)S(1)} %bitcast.222), kind=kOutput, calls=%fused_computation.81 | convolution fusion | flops 1074790400 | bytes 4194304 | tf_op jit(solution)/shard_map/scd,scf->df/dot_general | solution.py:87
  188.9 2.5 %pad_maximum_fusion.3 = bf16[2,1024,1024]{2,1,0:T(8,128)(2,1)} fusion(bf16[1,1024,1024]{2,1,0:T(8,128)(2,1)S(1)} %copy-done.2, bf16[1,1024,1024]{2,1,0:T(8,128)(2,1)S(1)} %copy-done.3), kind=kLoop, calls=%fused_computation.5 | loop fusion | flops 2097152 | bytes 8388608 | tf_op jit(solution)/shard_map/stack | solution.py:111
  193.2 3.7 %pad_maximum_fusion.1 = (bf16[2,1024,1024]{2,1,0:T(8,128)(2,1)}, bf16[2,1024,1024]{2,1,0:T(8,128)(2,1)}) fusion(bf16[1,1024,1024]{2,1,0:T(8,128)(2,1)S(1)} %copy-done.4, bf16[1,1024,1024]{2,1,0:T(8,128)(2,1)S(1)} %copy-done.5, bf16[1,1024,1024]{2,1,0:T(8,128)(2,1)S(1)} %copy-done.6, bf16[1,1024,1024]{2,1,0:T(8,128)(2,1)S(1)} %fusion.52), kind=kLoop, calls=%fused_computation.3 | loop fusion | flops 4194304 | bytes 16777216 | tf_op jit(solution)/shard_map/stack | solution.py:109
  197.8 2.3 %gather_fusion.1 = f32[512]{0:T(512)S(1)} fusion(f32[1024]{0:T(1024)S(1)} %reshape.155, s32[1024]{0:T(1024)S(1)} %copy-done.11), kind=kCustom, calls=%fused_computation.1 | custom fusion | bytes 6144 | tf_op jit(solution)/shard_map/jit(_take)/gather | solution.py:100
  201.0 2.0 all-to-all-done.3
  204.9 2.2 %select_reduce_fusion = bf16[256,256]{1,0:T(8,128)(2,1)} fusion(f32[256,2,256]{2,1,0:T(2,128)S(1)} %gather.13, pred[256,2]{1,0:T(8,128)(4,1)S(1)} %get-tuple-element.21), kind=kLoop, calls=%fused_computation.97 | loop fusion | flops 196608 | bytes 655872 | tf_op jit(solution)/shard_map/reduce_sum | solution.py:105
  (92 shorter events, 21.2 us)
Async XLA Ops:
  7.2 3.1 %copy-start = (bf16[256,2]{0,1:T(2,128)(2,1)S(1)}, bf16[256,2]{0,1:T(2,128)(2,1)}, u32[]{:S(2)}) copy-start(bf16[256,2]{0,1:T(2,128)(2,1)} %param.9) | copy-start | bytes 3076
  7.2 14.1 %copy-start.9 = (bf16[256,256]{1,0:T(8,128)(2,1)S(1)}, bf16[256,256]{1,0:T(8,128)(2,1)}, u32[]{:S(2)}) copy-start(bf16[256,256]{1,0:T(8,128)(2,1)} %param.7) | copy-start | bytes 393220
  10.1 1.3 copy-start.7
  11.4 23.0 %all-to-all-start = ((bf16[32,1,32]{2,1,0:T(2,128)(2,1)}), bf16[32,1,32]{2,1,0:T(2,128)(2,1)S(1)}, u32[]{:S(2)}, u32[]{:S(2)}) async-start(bf16[32,1,32]{2,1,0:T(2,128)(2,1)} %all_to_all.24), calls=%async_computation | async-start | bytes 32768 | tf_op jit(solution)/shard_map/all_to_all | solution.py:41
  34.4 9.7 %copy-start.10 = (bf16[256,256]{1,0:T(8,128)(2,1)S(1)}, bf16[256,256]{1,0:T(8,128)(2,1)}, u32[]{:S(2)}) copy-start(bf16[256,256]{1,0:T(8,128)(2,1)} %param.8) | copy-start | bytes 393220
  34.5 38.1 %all-to-all-start.2 = ((bf16[32,32,1024]{2,1,0:T(8,128)(2,1)}), bf16[32,32,1024]{2,1,0:T(8,128)(2,1)S(1)}, u32[]{:S(2)}, u32[]{:S(2)}) async-start(bf16[32,32,1024]{2,1,0:T(8,128)(2,1)} %bitcast.10), calls=%async_computation.2 | async-start | bytes 4194304 | tf_op jit(solution)/shard_map/all_to_all | solution.py:39
  72.5 33.6 %all-to-all-start.1 = ((bf16[32,32,1024]{2,1,0:T(8,128)(2,1)}), bf16[32,32,1024]{2,1,0:T(8,128)(2,1)}, u32[]{:S(2)}, u32[]{:S(2)}) async-start(bf16[32,32,1024]{2,1,0:T(8,128)(2,1)} %bitcast.5), calls=%async_computation.1 | async-start | bytes 4194304 | tf_op jit(solution)/shard_map/all_to_all | solution.py:40
  77.7 98.5 %reduce-scatter.2.cloned.1.call-start = ((), (), s32[]{:S(2)}) async-start(), calls=%async_computation.6 | async-start | bytes 5242880 | tf_op jit(solution)/shard_map/reduce_scatter | solution.py:101
  78.9 4.3 %copy-start.12 = (bf16[2,1024,1024]{2,1,0:T(8,128)(2,1)S(1)}, bf16[2,1024,1024]{2,1,0:T(8,128)(2,1)}, u32[]{:S(2)}) copy-start(bf16[2,1024,1024]{2,1,0:T(8,128)(2,1)} %param.11) | copy-start | bytes 12582916
  106.2 3.4 %copy-start.14 = (bf16[2,1024,1024]{2,1,0:T(8,128)(2,1)S(1)}, bf16[2,1024,1024]{2,1,0:T(8,128)(2,1)}, u32[]{:S(2)}) copy-start(bf16[2,1024,1024]{2,1,0:T(8,128)(2,1)} %param.12) | copy-start | bytes 12582916
  106.2 3.8 %copy-start.19 = (f32[32,16,1024]{2,1,0:T(8,128)S(1)}, f32[32,16,1024]{2,1,0:T(8,128)}, u32[]{:S(2)}) copy-start(f32[32,16,1024]{2,1,0:T(8,128)} %fusion.12) | copy-start | bytes 6291460
  110.0 4.0 %copy-start.13 = (bf16[2,1024,1024]{2,1,0:T(8,128)(2,1)S(1)}, bf16[2,1024,1024]{2,1,0:T(8,128)(2,1)}, u32[]{:S(2)}) copy-start(bf16[2,1024,1024]{2,1,0:T(8,128)(2,1)} %param.11) | copy-start | bytes 12582916
  113.0 1.0 copy-start.20
  114.0 2.2 %copy-start.15 = (bf16[2,1024,1024]{2,1,0:T(8,128)(2,1)S(1)}, bf16[2,1024,1024]{2,1,0:T(8,128)(2,1)}, u32[]{:S(2)}) copy-start(bf16[2,1024,1024]{2,1,0:T(8,128)(2,1)} %param.13) | copy-start | bytes 12582916
  116.2 2.7 %copy-start.18 = (f32[32,16,1024]{2,1,0:T(8,128)S(1)}, f32[32,16,1024]{2,1,0:T(8,128)}, u32[]{:S(2)}) copy-start(f32[32,16,1024]{2,1,0:T(8,128)} %fusion.24) | copy-start | bytes 6291460
  121.9 1.3 copy-start.21
  121.9 2.6 %copy-start.17 = (bf16[32,16,1024]{2,1,0:T(8,128)(2,1)}, bf16[32,16,1024]{2,1,0:T(8,128)(2,1)S(1)}, u32[]{:S(2)}) copy-start(bf16[32,16,1024]{2,1,0:T(8,128)(2,1)S(1)} %get-tuple-element.24) | copy-start | bytes 3145732
  128.6 3.7 %copy-start.16 = (bf16[2,1024,1024]{2,1,0:T(8,128)(2,1)S(1)}, bf16[2,1024,1024]{2,1,0:T(8,128)(2,1)}, u32[]{:S(2)}) copy-start(bf16[2,1024,1024]{2,1,0:T(8,128)(2,1)} %param.13) | copy-start | bytes 12582916
  128.6 3.7 %copy-start.24 = (bf16[32,16,1024]{2,1,0:T(8,128)(2,1)S(1)}, bf16[32,16,1024]{2,1,0:T(8,128)(2,1)}, u32[]{:S(2)}) copy-start(bf16[32,16,1024]{2,1,0:T(8,128)(2,1)} %get-tuple-element.22) | copy-start | bytes 3145732
  151.9 26.7 %all-to-all-start.4 = ((f32[32,2,16]{2,1,0:T(2,128)}), f32[32,2,16]{2,1,0:T(2,128)}, u32[]{:S(2)}, u32[]{:S(2)}) async-start(f32[32,2,16]{2,1,0:T(2,128)} %psum.7), calls=%async_computation.5 | async-start | bytes 65536 | tf_op jit(solution)/shard_map/all_to_all | solution.py:98
  159.0 4.0 %copy-start.22 = (bf16[32,16,1024]{2,1,0:T(8,128)(2,1)S(1)}, bf16[32,16,1024]{2,1,0:T(8,128)(2,1)}, u32[]{:S(2)}) copy-start(bf16[32,16,1024]{2,1,0:T(8,128)(2,1)} %copy-done.21) | copy-start | bytes 3145732
  163.0 2.6 %copy-start.23 = (bf16[32,16,1024]{2,1,0:T(8,128)(2,1)S(1)}, bf16[32,16,1024]{2,1,0:T(8,128)(2,1)}, u32[]{:S(2)}) copy-start(bf16[32,16,1024]{2,1,0:T(8,128)(2,1)} %get-tuple-element.25) | copy-start | bytes 3145732
  165.7 4.0 %copy-start.25 = (bf16[32,16,1024]{2,1,0:T(8,128)(2,1)S(1)}, bf16[32,16,1024]{2,1,0:T(8,128)(2,1)}, u32[]{:S(2)}) copy-start(bf16[32,16,1024]{2,1,0:T(8,128)(2,1)} %get-tuple-element.22) | copy-start | bytes 3145732
  178.6 24.4 %all-to-all-start.3 = ((f32[32,2,16,256]{3,2,1,0:T(8,128)}), f32[32,2,16,256]{3,2,1,0:T(8,128)S(1)}, u32[]{:S(2)}, u32[]{:S(2)}) async-start(f32[32,2,16,256]{3,2,1,0:T(8,128)} %copy.82), calls=%async_computation.4 | async-start | bytes 2097152 | tf_op jit(solution)/shard_map/all_to_all | solution.py:102
  186.1 2.7 %copy-start.2 = (bf16[1,1024,1024]{2,1,0:T(8,128)(2,1)S(1)}, bf16[1,1024,1024]{2,1,0:T(8,128)(2,1)}, u32[]{:S(2)}) copy-start(bf16[1,1024,1024]{2,1,0:T(8,128)(2,1)} %fusion.55) | copy-start | bytes 6291460
  186.1 2.7 %copy-start.3 = (bf16[1,1024,1024]{2,1,0:T(8,128)(2,1)S(1)}, bf16[1,1024,1024]{2,1,0:T(8,128)(2,1)}, u32[]{:S(2)}) copy-start(bf16[1,1024,1024]{2,1,0:T(8,128)(2,1)} %fusion.54) | copy-start | bytes 6291460
  188.8 2.5 %copy-start.4 = (bf16[1,1024,1024]{2,1,0:T(8,128)(2,1)S(1)}, bf16[1,1024,1024]{2,1,0:T(8,128)(2,1)}, u32[]{:S(2)}) copy-start(bf16[1,1024,1024]{2,1,0:T(8,128)(2,1)} %fusion.51) | copy-start | bytes 6291460
  188.8 3.7 %copy-start.5 = (bf16[1,1024,1024]{2,1,0:T(8,128)(2,1)S(1)}, bf16[1,1024,1024]{2,1,0:T(8,128)(2,1)}, u32[]{:S(2)}) copy-start(bf16[1,1024,1024]{2,1,0:T(8,128)(2,1)} %fusion.50) | copy-start | bytes 6291460
  188.9 4.4 %copy-start.6 = (bf16[1,1024,1024]{2,1,0:T(8,128)(2,1)S(1)}, bf16[1,1024,1024]{2,1,0:T(8,128)(2,1)}, u32[]{:S(2)}) copy-start(bf16[1,1024,1024]{2,1,0:T(8,128)(2,1)} %fusion.53) | copy-start | bytes 6291460
  193.2 4.6 %copy-start.11 = (s32[1024]{0:T(1024)S(1)}, s32[1024]{0:T(1024)}, u32[]{:S(2)}) copy-start(s32[1024]{0:T(1024)} %pad_clamp_fusion) | copy-start | bytes 12292
  196.9 3.3 %copy-start.8 = (s32[256,2]{1,0:T(8,128)S(1)}, s32[256,2]{1,0:T(8,128)}, u32[]{:S(2)}) copy-start(s32[256,2]{1,0:T(8,128)} %copy-done.7) | copy-start | bytes 6148
  203.0 4.0 %copy-start.1 = (bf16[256,2]{0,1:T(2,128)(2,1)S(1)}, bf16[256,2]{0,1:T(2,128)(2,1)}, u32[]{:S(2)}) copy-start(bf16[256,2]{0,1:T(2,128)(2,1)} %param.9) | copy-start | bytes 3076
Sparse Core Ops, SparseCore 0:
  128.7 44.9 reduce-scatter.1
where the time goes:
time: 215 us; the launch traced here: 214 us
  matrix products  55 us (26%)
  blocking collectives  39.6 us (18%)
  starting transfers between devices  39.1 us (18%)
  waiting for transfers between devices  37.1 us (17%)
  local copies, waits for them, and re-layouts  15.2 us (7%)
  between operations  14.4 us (7%)
  other arithmetic  13.4 us (6%)
    all_to_all x1, waiting for transfers between devices, on_device(): lax.all_to_all(send_dy, 'dp', split_axis=0, concat_axis=0, tiled=True)  20.3 us
    psum x1, blocking collectives, on_device(): gate_total = lax.psum(gate_stack, 'mp')  17 us
    all_to_all x1, waiting for transfers between devices, on_device(): lax.all_to_all(send_x, 'dp', split_axis=0, concat_axis=0, tiled=True)  14.8 us
    all_gather x1, blocking collectives, on_device(): lax.all_gather(grad_out, 'mp', axis=1, tiled=True)  11.5 us
    all_gather x1, blocking collectives, on_device(): lax.all_gather(tokens, 'mp', axis=1, tiled=True)  11.1 us
    all_to_all x1, starting transfers between devices, on_device(): lax.all_to_all(send_x, 'dp', split_axis=0, concat_axis=0, tiled=True)  9.72 us
    all_to_all x1, starting transfers between devices, on_device(): lax.all_to_all(slot_gate, 'dp', split_axis=0, concat_axis=0, tiled=True)  9.42 us
    dot_general x2, matrix products, on_device(): jnp.einsum('scf,scd->fd', hidden, scaled, preferred_element_type=jnp.floa...  7.93 us
  transfers between devices with their start and end apart: 6, of which 3 were waited for; matrix products, arithmetic and copies ran while one was open for 24% of the time, Pallas kernels for 0%

commit v1 on v0

v1 whole, which is shorter than its diff:
```python
import functools

import jax
import jax.numpy as jnp
from jax import lax
from jax.experimental import pallas as pl
from jax.experimental.pallas import tpu as pltpu
from jax.sharding import PartitionSpec as P

F32 = jnp.float32
BF16 = jnp.bfloat16
MESH = pl.DeviceIdType.MESH
RING = 4
GROUPS = 32
CAP = 16
LOCAL = 2
ROWS = GROUPS * CAP
TOK = 256
D = 1024
Q = 256
F = 1024
STEP = 256
PART = 128


def dot(a, b, contract):
    return lax.dot_general(a, b, ((contract[0], contract[1]), ((), ())), preferred_element_type=F32)


def peer(k, sign):
    me = lax.axis_index("dp")
    x, z, c = me // 8, (me // 2) % 4, me % 2
    dx, dz, dc = k // 8, (k // 2) % 4, k % 2
    x = (x + sign * dx + RING) % RING
    z = (z + sign * dz + RING) % RING
    c = (c + dc) % 2
    return x * 8 + z * 2 + c


def columns(q):
    return pl.ds(pl.multiple_of(q * Q, Q), Q)


def tile(j, size):
    return pl.ds(pl.multiple_of(j * size, size), size)


def local_wait(ref, sem):
    pltpu.make_async_copy(ref, ref, sem).wait()


def kernel(
    ids_ref, gates_ref, tokens_ref, dy_ref, wg_hbm, wu_hbm, wd_hbm,
    out_ref, gg_ref, gw_ref, uw_ref, dw_ref,
    wg, wu, wd, route, send, xs, pre_g, pre_u, pre_h, hid, dgate, dup,
    pa, pb, ra, rb, red, ret, back, gp, gt, gb, gl, gr, grad,
    w_sem, send_sem, a2a_sem, left_sem, right_sem, lf_sem, rf_sem,
    ra_sem, rb_sem, back_sem, gb_sem, gr_sem, out_sem,
):
    me = lax.axis_index("dp")
    y = lax.axis_index("mp")
    right, left, across = (y + 1) % RING, (y + 3) % RING, (y + 2) % RING
    barrier = pltpu.get_barrier_semaphore()

    def greet(k, _):
        pl.semaphore_signal(barrier, inc=1, device_id=(peer(k, 1), y), device_id_type=MESH)
        return 0

    lax.fori_loop(1, GROUPS, greet, 0)
    for other in (right, left, across):
        pl.semaphore_signal(barrier, inc=1, device_id=(me, other), device_id_type=MESH)

    loads = []
    for e in range(LOCAL):
        for i, (src, dst) in enumerate(((wg_hbm, wg), (wu_hbm, wu), (wd_hbm, wd))):
            copy = pltpu.make_async_copy(src.at[e], dst.at[e], w_sem.at[e, i])
            copy.start()
            loads.append(copy)

    expert_iota = lax.broadcasted_iota(jnp.int32, (LOCAL * GROUPS, TOK), 0)
    named = [(expert_iota == ids_ref[j : j + 1, :]).astype(F32) for j in range(2)]
    earlier = (
        lax.broadcasted_iota(jnp.int32, (TOK, TOK), 0) < lax.broadcasted_iota(jnp.int32, (TOK, TOK), 1)
    ).astype(F32)
    before = dot((named[0] + named[1]).astype(BF16), earlier.astype(BF16), ((1,), (0,)))
    x_me, z_me, c_me = me // 8, (me // 2) % 4, me % 2
    slot_iota = lax.broadcasted_iota(jnp.int32, (LOCAL * ROWS, TOK), 0)
    picks = []
    for j in range(2):
        position = jnp.sum(before * named[j], axis=0, keepdims=True).astype(jnp.int32)
        expert = ids_ref[j : j + 1, :]
        group = expert >> 1
        k = ((((group >> 3) - x_me) & 3) * 4 + ((((group >> 1) & 3) - z_me) & 3)) * 2 + (((group & 1) - c_me) & 1)
        slot = (expert & 1) * ROWS + k * CAP + position
        pick = (slot_iota == slot).astype(F32)
        route[j] = pick.astype(BF16)
        picks.append(pick)
    send_x = dot((picks[0] + picks[1]).astype(BF16), tokens_ref[...], ((1,), (0,)))
    weighted = (picks[0] * gates_ref[0:1, :] + picks[1] * gates_ref[1:2, :]).astype(BF16)
    send_s = dot(weighted, dy_ref[...], ((1,), (0,)))
    for e in range(LOCAL):
        send[0, e] = send_x[e * ROWS : (e + 1) * ROWS].astype(BF16)
        send[1, e] = send_s[e * ROWS : (e + 1) * ROWS].astype(BF16)

    pl.semaphore_wait(barrier, GROUPS - 1 + 3)

    own = columns(y)
    for e in range(LOCAL):
        pltpu.make_async_copy(
            send.at[:, e, pl.ds(0, CAP), :], xs.at[:, e, pl.ds(0, CAP), own], a2a_sem.at[e, 0]
        ).start()
        for g in range(RING):

            def dispatch(k, _):
                rows = tile(k, CAP)
                pltpu.make_async_remote_copy(
                    src_ref=send.at[:, e, rows, :],
                    dst_ref=xs.at[:, e, rows, own],
                    send_sem=send_sem.at[0],
                    recv_sem=a2a_sem.at[e, g],
                    device_id=(peer(k, 1), y),
                    device_id_type=MESH,
                ).start()
                return 0

            lax.fori_loop(max(1, g * 8), g * 8 + 8, dispatch, 0)

    def share(e, g):
        rows = pl.ds(g * PART, PART)
        local_wait(xs.at[:, e, rows, own], a2a_sem.at[e, g])
        for other, arrive, s in ((right, left_sem, 1), (left, right_sem, 2)):
            pltpu.make_async_remote_copy(
                src_ref=xs.at[:, e, rows, own],
                dst_ref=xs.at[:, e, rows, own],
                send_sem=send_sem.at[s],
                recv_sem=arrive.at[e, g],
                device_id=(me, other),
                device_id_type=MESH,
            ).start()

    def forward(e, g):
        rows = pl.ds(g * PART, PART)
        for origin, arrived, arrive, other, array, s in (
            (left, left_sem, lf_sem, right, 0, 3),
            (right, right_sem, rf_sem, left, 1, 4),
        ):
            cols = columns(origin)
            local_wait(xs.at[:, e, rows, cols], arrived.at[e, g])
            pltpu.make_async_remote_copy(
                src_ref=xs.at[array, e, rows, cols],
                dst_ref=xs.at[array, e, rows, cols],
                send_sem=send_sem.at[s],
                recv_sem=arrive.at[e, g],
                device_id=(me, other),
                device_id_type=MESH,
            ).start()

    def arrive_all(e):
        cols = columns(across)
        for g in range(RING):
            rows = pl.ds(g * PART, PART)
            local_wait(xs.at[0, e, rows, cols], lf_sem.at[e, g])
            local_wait(xs.at[1, e, rows, cols], rf_sem.at[e, g])

    def hidden_tiles(e, start, stop):
        def body(j, _):
            cols = tile(j, STEP)
            pre_g[...] = dot(xs[0, e], wg[e, :, cols], ((1,), (0,)))
            pre_u[...] = dot(xs[0, e], wu[e, :, cols], ((1,), (0,)))
            pre_h[...] = dot(xs[1, e], wd[e, cols, :], ((1,), (1,)))

            def rows_body(i, _):
                rows = tile(i, 64)
                g, u, dh = pre_g[rows, :], pre_u[rows, :], pre_h[rows, :]
                s = jax.nn.sigmoid(g)
                act = g * s
                h = (act * u).astype(BF16)
                hid[e, rows, cols] = h
                dgate[e, rows, cols] = (dh * u * s * (1.0 + g * (1.0 - s))).astype(BF16)
                dup[e, rows, cols] = (dh * act).astype(BF16)
                product = h.astype(F32) * dh
                gp[e, rows, :] += product[:, :128] + product[:, 128:]
                return 0

            lax.fori_loop(0, ROWS // 64, rows_body, 0)
            return 0

        lax.fori_loop(start, stop, body, 0)

    def dx_tile(e, q):
        rows = columns(q)
        return dot(dgate[e], wg[e, rows, :], ((1,), (1,))) + dot(dup[e], wu[e, rows, :], ((1,), (1,)))

    def ring_copy(src, dst, s, sem, other):
        pltpu.make_async_remote_copy(
            src_ref=src, dst_ref=dst, send_sem=send_sem.at[s], recv_sem=sem, device_id=(me, other), device_id_type=MESH
        ).start()

    half = ROWS // 2

    def reduce_first(e):
        pa[e] = dx_tile(e, across).astype(BF16)
        ring_copy(pa.at[e, pl.ds(0, half)], ra.at[e, 0], 5, ra_sem.at[e, 0], right)
        ring_copy(pa.at[e, pl.ds(half, half)], ra.at[e, 1], 5, ra_sem.at[e, 1], left)

    def reduce_second(e):
        pre_g[...] = dx_tile(e, right)
        local_wait(ra.at[e, 0], ra_sem.at[e, 0])
        pb[e, 0, :half] = (pre_g[:half] + ra[e, 0].astype(F32)).astype(BF16)
        pb[e, 0, half:] = pre_g[half:].astype(BF16)
        ring_copy(pb.at[e, 0], rb.at[e, 0], 6, rb_sem.at[e, 0], right)
        pre_g[...] = dx_tile(e, left)
        local_wait(ra.at[e, 1], ra_sem.at[e, 1])
        pb[e, 1, :half] = pre_g[:half].astype(BF16)
        pb[e, 1, half:] = (pre_g[half:] + ra[e, 1].astype(F32)).astype(BF16)
        ring_copy(pb.at[e, 1], rb.at[e, 1], 6, rb_sem.at[e, 1], left)
        red[e] = dx_tile(e, y)

    def give_back(e):
        local_wait(rb.at[e, 0], rb_sem.at[e, 0])
        local_wait(rb.at[e, 1], rb_sem.at[e, 1])
        ret[e] = (red[e] + rb[e, 0].astype(F32) + rb[e, 1].astype(F32)).astype(BF16)
        pltpu.make_async_copy(ret.at[e, pl.ds(0, CAP), :], back.at[e, pl.ds(0, CAP), :], back_sem.at[e]).start()

        def body(k, _):
            rows = tile(k, CAP)
            pltpu.make_async_remote_copy(
                src_ref=ret.at[e, rows, :],
                dst_ref=back.at[e, rows, :],
                send_sem=send_sem.at[7],
                recv_sem=back_sem.at[e],
                device_id=(peer(k, -1), y),
                device_id_type=MESH,
            ).start()
            return 0

        lax.fori_loop(1, GROUPS, body, 0)

    def weight_tiles(e, which, start, stop):
        rows_of, others, result, number = (
            (xs.at[0, e], dgate.at[e], gw_ref, 0),
            (xs.at[0, e], dup.at[e], uw_ref, 1),
            (hid.at[e], xs.at[1, e], dw_ref, 2),
        )[which]

        def body(j, _):
            cols = tile(j, STEP)
            grad[number, cols, :] = dot(rows_of[:, cols], others[...], ((0,), (0,))).astype(BF16)
            pltpu.make_async_copy(grad.at[number, cols, :], result.at[e, cols, :], out_sem.at[e, which]).start()
            return 0

        lax.fori_loop(start, stop, body, 0)

    def weights_wait(e):
        for which, result in enumerate((gw_ref, uw_ref, dw_ref)):
            local_wait(result.at[e], out_sem.at[e, which])

    def gates_back():
        lanes = lax.broadcasted_iota(jnp.int32, (ROWS, 128), 1)
        high, low = [], []
        for e in range(LOCAL):
            total = jnp.sum(gp[e], axis=1, keepdims=True)
            upper = total.astype(BF16).astype(F32)
            high.append(upper)
            low.append(total - upper)
        gt[...] = jnp.where(
            lanes < 32, high[0], jnp.where(lanes < 64, low[0], jnp.where(lanes < 96, high[1], low[1]))
        ).astype(BF16)
        pltpu.make_async_copy(gt.at[pl.ds(0, CAP), :], gb.at[pl.ds(0, CAP), :], gb_sem).start()

        def body(k, _):
            rows = tile(k, CAP)
            pltpu.make_async_remote_copy(
                src_ref=gt.at[rows, :],
                dst_ref=gb.at[rows, :],
                send_sem=send_sem.at[8],
                recv_sem=gb_sem,
                device_id=(peer(k, -1), y),
                device_id_type=MESH,
            ).start()
            return 0

        lax.fori_loop(1, GROUPS, body, 0)

    def gates_share():
        local_wait(gb, gb_sem)
        for j in range(2):
            first = dot(gb[...], route[j, :ROWS], ((0,), (0,)))
            second = dot(gb[...], route[j, ROWS:], ((0,), (0,)))
            gl[j : j + 1, :] = (first[0:1] + first[32:33]) + (second[64:65] + second[96:97])
        for i, other in enumerate((right, left, across)):
            ring_copy(gl, gr.at[i], 9, gr_sem.at[i], other)

    def gates_finish():
        for i in range(3):
            local_wait(gr.at[i], gr_sem.at[i])
        total = gl[0:2, :] + gr[0, 0:2, :] + gr[1, 0:2, :] + gr[2, 0:2, :]
        gg_ref[...] = total / gates_ref[...]

    gp[...] = jnp.zeros_like(gp)
    gl[...] = jnp.zeros_like(gl)

    for g in range(RING):
        share(0, g)
    for g in range(RING):
        forward(0, g)
    for g in range(RING):
        share(1, g)
    arrive_all(0)
    for copy in loads[:3]:
        copy.wait()
    hidden_tiles(0, 0, 3)
    forward(1, 0)
    hidden_tiles(0, 3, 4)
    reduce_first(0)
    weight_tiles(0, 0, 0, 2)
    forward(1, 1)
    reduce_second(0)
    forward(1, 2)
    weight_tiles(0, 0, 2, 4)
    weight_tiles(0, 1, 0, 4)
    forward(1, 3)
    give_back(0)
    weight_tiles(0, 2, 0, 4)
    arrive_all(1)
    for copy in loads[3:]:
        copy.wait()
    weights_wait(0)
    hidden_tiles(1, 0, 4)
    gates_back()
    reduce_first(1)
    weight_tiles(1, 0, 0, 2)
    reduce_second(1)
    gates_share()
    weight_tiles(1, 0, 2, 4)
    weight_tiles(1, 1, 0, 4)
    give_back(1)
    weight_tiles(1, 2, 0, 4)
    gates_finish()

    local_wait(back.at[0], back_sem.at[0])
    local_wait(back.at[1], back_sem.at[1])
    both = (route[0].astype(F32) + route[1].astype(F32)).astype(BF16)
    out_ref[...] = (
        dot(both[:ROWS], back[0], ((0,), (0,))) + dot(both[ROWS:], back[1], ((0,), (0,)))
    ).astype(BF16)

    weights_wait(1)
    local_wait(send.at[:, :, pl.ds(CAP, ROWS - CAP), :], send_sem.at[0])
    for s in (1, 2):
        local_wait(xs.at[:, :, :, own], send_sem.at[s])
    for s in (3, 4):
        local_wait(xs.at[0, :, :, own], send_sem.at[s])
    local_wait(pa, send_sem.at[5])
    local_wait(pb, send_sem.at[6])
    local_wait(ret.at[:, pl.ds(CAP, ROWS - CAP), :], send_sem.at[7])
    local_wait(gt.at[pl.ds(CAP, ROWS - CAP), :], send_sem.at[8])
    local_wait(gr, send_sem.at[9])


def on_device(tokens, grad_out, gates, expert_ids, w_gate, w_up, w_down):
    vmem = pl.BlockSpec(memory_space=pltpu.VMEM)
    hbm = pl.BlockSpec(memory_space=pl.ANY)
    weight = jax.ShapeDtypeStruct((LOCAL, D, F), BF16)
    dma = pltpu.SemaphoreType.DMA
    grad_tokens, grad_gates, grad_gate, grad_up, grad_down = pl.pallas_call(
        kernel,
        name="expert_layer",
        out_shape=(
            jax.ShapeDtypeStruct((TOK, Q), BF16),
            jax.ShapeDtypeStruct((2, TOK), F32),
            weight,
            weight,
            weight,
        ),
        in_specs=[vmem, vmem, vmem, vmem, hbm, hbm, hbm],
        out_specs=(vmem, vmem, hbm, hbm, hbm),
        scratch_shapes=[
            pltpu.VMEM((LOCAL, D, F), BF16),
            pltpu.VMEM((LOCAL, D, F), BF16),
            pltpu.VMEM((LOCAL, F, D), BF16),
            pltpu.VMEM((2, LOCAL * ROWS, TOK), BF16),
            pltpu.VMEM((2, LOCAL, ROWS, Q), BF16),
            pltpu.VMEM((2, LOCAL, ROWS, D), BF16),
            pltpu.VMEM((ROWS, STEP), F32),
            pltpu.VMEM((ROWS, STEP), F32),
            pltpu.VMEM((ROWS, STEP), F32),
            pltpu.VMEM((LOCAL, ROWS, F), BF16),
            pltpu.VMEM((LOCAL, ROWS, F), BF16),
            pltpu.VMEM((LOCAL, ROWS, F), BF16),
            pltpu.VMEM((LOCAL, ROWS, Q), BF16),
            pltpu.VMEM((LOCAL, 2, ROWS, Q), BF16),
            pltpu.VMEM((LOCAL, 2, ROWS // 2, Q), BF16),
            pltpu.VMEM((LOCAL, 2, ROWS, Q), BF16),
            pltpu.VMEM((LOCAL, ROWS, Q), F32),
            pltpu.VMEM((LOCAL, ROWS, Q), BF16),
            pltpu.VMEM((LOCAL, ROWS, Q), BF16),
            pltpu.VMEM((LOCAL, ROWS, 128), F32),
            pltpu.VMEM((ROWS, 128), BF16),
            pltpu.VMEM((ROWS, 128), BF16),
            pltpu.VMEM((8, TOK), F32),
            pltpu.VMEM((3, 8, TOK), F32),
            pltpu.VMEM((3, D, F), BF16),
            dma((LOCAL, 3)),
            dma((10,)),
            dma((LOCAL, RING)),
            dma((LOCAL, RING)),
            dma((LOCAL, RING)),
            dma((LOCAL, RING)),
            dma((LOCAL, RING)),
            dma((LOCAL, 2)),
            dma((LOCAL, 2)),
            dma((LOCAL,)),
            dma,
            dma((3,)),
            dma((LOCAL, 3)),
        ],
        compiler_params=pltpu.CompilerParams(
            collective_id=0, has_side_effects=True, vmem_limit_bytes=60 * 1024 * 1024
        ),
    )(expert_ids.T, gates.T.astype(F32), tokens, grad_out, w_gate, w_up, w_down)
    return grad_tokens, grad_gates.T, grad_gate, grad_up, grad_down


def solution(mesh):
    placed = (
        P("dp", "mp"),
        P("dp", "mp"),
        P("dp", None),
        P("dp", None),
        P("dp", None, "mp"),
        P("dp", None, "mp"),
        P("dp", "mp", None),
    )
    return jax.shard_map(
        on_device,
        mesh=mesh,
        in_specs=placed,
        out_specs=(
            P("dp", "mp"),
            P("dp", None),
            P("dp", None, "mp"),
            P("dp", None, "mp"),
            P("dp", "mp", None),
        ),
        check_vma=False,
    )
```

time: 215 us -> 108 us (0.50)
  Pallas kernels: 0 us -> 93 us
  matrix products: 55 us -> 0 us
  blocking collectives: 39.6 us -> 0 us
  starting transfers between devices: 39.1 us -> 0 us
  waiting for transfers between devices: 37.1 us -> 0 us
  between operations: 14.4 us -> 0.64 us
  other arithmetic: 13.4 us -> 1.26 us
    pallas_call x0 -> x1, Pallas kernels: none -> 93 us  [on_device(): pl.pallas_call(kernel, name='expert_layer', out_shape=(jax.ShapeDtypeStru...]
    dot_general x21 -> x0, matrix products: 55 us -> none  [the longest x2 7.93 us: on_device(): jnp.einsum('scf,scd->fd', hidden, scaled, preferred_element_type=jnp.floa...]
    all_to_all x5 -> x0, starting transfers between devices: 38.9 us -> none  [the longest x1 9.72 us: on_device(): lax.all_to_all(send_x, 'dp', split_axis=0, concat_axis=0, tiled=True)]
    all_to_all x5 -> x0, waiting for transfers between devices: 37.1 us -> none  [the longest x1 20.3 us: on_device(): lax.all_to_all(send_dy, 'dp', split_axis=0, concat_axis=0, tiled=True)]
    all_gather x2 -> x0, blocking collectives: 22.6 us -> none  [the longest x1 11.5 us: on_device(): lax.all_gather(grad_out, 'mp', axis=1, tiled=True)]
    psum x1 -> x0, blocking collectives: 17 us -> none  [on_device(): gate_total = lax.psum(gate_stack, 'mp')]
    another operation x6 -> x0, other arithmetic: 9.99 us -> none  [the longest x1 3.69 us: on_device(): jnp.stack(grads_gate, axis=0)]
    unnamed x54 -> x9, local copies, waits for them, and re-layouts: 5.84 us -> 13.3 us
  transfers between devices with their start and end apart: 6 -> 0, of which waited for: 3 -> 0; matrix products, arithmetic and copies ran while one was open for 24% -> 0% of each run, Pallas kernels for 0% -> 0%
where the time goes in v1:
time: 108 us
  Pallas kernels  93 us (86%)
  local copies, waits for them, and re-layouts  13.3 us (12%)
  other arithmetic  1.26 us (1%)
    pallas_call x1, Pallas kernels, on_device(): pl.pallas_call(kernel, name='expert_layer', out_shape=(jax.ShapeDtypeStru...  93 us
    unnamed x9, local copies, waits for them, and re-layouts  13.3 us

profile of v1, /device:TPU:1, one launch (start us, length us, event | category | flops | bytes accessed | tf_op | source)
XLA Modules:
  0.0 108.2 jit_solution(1740436034359564807)
XLA Ops:
  0.6 1.3 %convert_bitcast_fusion.gates_ref = f32[2,256]{1,0:T(2,128)} fusion(bf16[256,2]{0,1:T(2,128)(2,1)} %param.9), kind=kLoop, calls=%fused_computation | loop fusion | flops 512 | bytes 3072 | tf_op jit(solution)/shard_map/convert_element_type | solution.py:421
  1.9 93.0 %expert_layer.1 = (bf16[256,256]{1,0:T(8,128)(2,1)}, f32[2,256]{1,0:T(2,128)}, bf16[2,1024,1024]{2,1,0:T(8,128)(2,1)}, bf16[2,1024,1024]{2,1,0:T(8,128)(2,1)}, bf16[2,1024,1024]{2,1,0:T(8,128)(2,1)}) custom-call(s32[2,256]{1,0:T(2,128)} %bitcast.4, f32[2,256]{1,0:T(2,128)} %convert_bitcast_fusion.gates_ref, bf16[256,256]{1,0:T(8,128)(2,1)} %tokens_ref.1, ...), custom_call_target="tpu_custom_call" | custom-call | tf_op jit(solution)/shard_map/expert_layer/pallas_call | solution.py:366
  94.9 1.6 %copy.17 = bf16[256,256]{1,0:T(8,128)(2,1)} copy(bf16[256,256]{1,0:T(8,128)(2,1)} %get-tuple-element.20) | data formatting | bytes 262144
  96.5 1.2 %copy.18 = f32[256,2]{0,1:T(2,128)} copy(f32[256,2]{0,1:T(2,128)} %bitcast.5) | data formatting | bytes 4096
  97.7 0.0 copy-start.1
  97.7 4.8 %copy.19 = bf16[2,1024,1024]{2,1,0:T(8,128)(2,1)} copy(bf16[2,1024,1024]{2,1,0:T(8,128)(2,1)} %get-tuple-element.22) | data formatting | bytes 8388608
  102.5 0.0 copy-done.1
  102.5 0.0 copy-start
  102.5 2.1 %copy.20 = bf16[2,1024,1024]{2,1,0:T(8,128)(2,1)} copy(bf16[2,1024,1024]{2,1,0:T(8,128)(2,1)S(1)} %copy-done.1) | data formatting | bytes 8388608
  104.6 1.6 %copy-done = bf16[2,1024,1024]{2,1,0:T(8,128)(2,1)S(1)} copy-done((bf16[2,1024,1024]{2,1,0:T(8,128)(2,1)S(1)}, bf16[2,1024,1024]{2,1,0:T(8,128)(2,1)}, u32[]{:S(2)}) %copy-start) | copy-done | bytes 4194328
  106.2 2.0 %copy.21 = bf16[2,1024,1024]{2,1,0:T(8,128)(2,1)} copy(bf16[2,1024,1024]{2,1,0:T(8,128)(2,1)S(1)} %copy-done) | data formatting | bytes 8388608
Async XLA Ops:
  97.7 4.8 %copy-start.1 = (bf16[2,1024,1024]{2,1,0:T(8,128)(2,1)S(1)}, bf16[2,1024,1024]{2,1,0:T(8,128)(2,1)}, u32[]{:S(2)}) copy-start(bf16[2,1024,1024]{2,1,0:T(8,128)(2,1)} %get-tuple-element.23) | copy-start | bytes 12582916
  102.5 3.7 %copy-start = (bf16[2,1024,1024]{2,1,0:T(8,128)(2,1)S(1)}, bf16[2,1024,1024]{2,1,0:T(8,128)(2,1)}, u32[]{:S(2)}) copy-start(bf16[2,1024,1024]{2,1,0:T(8,128)(2,1)} %get-tuple-element.24) | copy-start | bytes 12582916

commit v2 on v1

--- a/solution.py
+++ b/solution.py
@@ -19,6 +19,7 @@
 D = 1024
 Q = 256
 F = 1024
+LANES = 128
 STEP = 256
 PART = 128
 
@@ -30,7 +31,8 @@
 def peer(k, sign):
     me = lax.axis_index("dp")
     x, z, c = me // 8, (me // 2) % 4, me % 2
-    dx, dz, dc = k // 8, (k // 2) % 4, k % 2
+    dx = (k // 2) % 4
+    dz, dc = (dx + k // 8) % 4, k % 2
     x = (x + sign * dx + RING) % RING
     z = (z + sign * dz + RING) % RING
     c = (c + dc) % 2
@@ -52,10 +54,10 @@
 def kernel(
     ids_ref, gates_ref, tokens_ref, dy_ref, wg_hbm, wu_hbm, wd_hbm,
     out_ref, gg_ref, gw_ref, uw_ref, dw_ref,
-    wg, wu, wd, route, send, xs, pre_g, pre_u, pre_h, hid, dgate, dup,
-    pa, pb, ra, rb, red, ret, back, gp, gt, gb, gl, gr, grad,
-    w_sem, send_sem, a2a_sem, left_sem, right_sem, lf_sem, rf_sem,
-    ra_sem, rb_sem, back_sem, gb_sem, gr_sem, out_sem,
+    wg, wu, wd, route, gated, late, early, dys, pan, sf, pre_g, pre_u, pre_h, hid, dgate, dup,
+    pa, pb, ra, rb, red, ret, back, gp, gt, gb, gl, gr,
+    w_sem, send_sem, late_sem, early_sem, dy_sem, left_sem, right_sem, lf_sem, rf_sem,
+    ra_sem, rb_sem, back_sem, gb_sem, gr_sem,
 ):
     me = lax.axis_index("dp")
     y = lax.axis_index("mp")
@@ -77,6 +79,7 @@
             copy.start()
             loads.append(copy)
 
+    gate_rows = gates_ref[...].astype(F32)
     expert_iota = lax.broadcasted_iota(jnp.int32, (LOCAL * GROUPS, TOK), 0)
     named = [(expert_iota == ids_ref[j : j + 1, :]).astype(F32) for j in range(2)]
     earlier = (
@@ -90,48 +93,107 @@
         position = jnp.sum(before * named[j], axis=0, keepdims=True).astype(jnp.int32)
         expert = ids_ref[j : j + 1, :]
         group = expert >> 1
-        k = ((((group >> 3) - x_me) & 3) * 4 + ((((group >> 1) & 3) - z_me) & 3)) * 2 + (((group & 1) - c_me) & 1)
+        dx = ((group >> 3) - x_me) & 3
+        dz = ((group >> 1) - z_me) & 3
+        k = ((dz - dx) & 3) * 8 + dx * 2 + (((group & 1) - c_me) & 1)
         slot = (expert & 1) * ROWS + k * CAP + position
         pick = (slot_iota == slot).astype(F32)
         route[j] = pick.astype(BF16)
         picks.append(pick)
     send_x = dot((picks[0] + picks[1]).astype(BF16), tokens_ref[...], ((1,), (0,)))
-    weighted = (picks[0] * gates_ref[0:1, :] + picks[1] * gates_ref[1:2, :]).astype(BF16)
-    send_s = dot(weighted, dy_ref[...], ((1,), (0,)))
+    weighted = (picks[0] * gate_rows[0:1, :] + picks[1] * gate_rows[1:2, :]).astype(BF16)
+    gated[...] = weighted
+    send_s = dot(weighted, dy_ref[:, LANES:], ((1,), (0,)))
     for e in range(LOCAL):
-        send[0, e] = send_x[e * ROWS : (e + 1) * ROWS].astype(BF16)
-        send[1, e] = send_s[e * ROWS : (e + 1) * ROWS].astype(BF16)
+        rows = slice(e * ROWS, (e + 1) * ROWS)
+        late[e, 0] = send_x[rows, :LANES].astype(BF16)
+        late[e, 1] = send_x[rows, LANES:].astype(BF16)
+        late[e, 2] = send_s[rows].astype(BF16)
 
     pl.semaphore_wait(barrier, GROUPS - 1 + 3)
 
-    own = columns(y)
-    for e in range(LOCAL):
+    def tokens_copy(src, origin, rows, sem, other):
+        pltpu.make_async_remote_copy(
+            src_ref=src,
+            dst_ref=dys.at[origin, rows, :],
+            send_sem=send_sem.at[10],
+            recv_sem=sem,
+            device_id=(me, other),
+            device_id_type=MESH,
+        ).start()
+
+    everyone = pl.ds(0, TOK)
+    pltpu.make_async_copy(dy_ref.at[:, pl.ds(0, LANES)], dys.at[y], dy_sem.at[0]).start()
+    tokens_copy(dy_ref.at[:, pl.ds(0, LANES)], y, everyone, dy_sem.at[1], right)
+    tokens_copy(dy_ref.at[:, pl.ds(0, LANES)], y, everyone, dy_sem.at[2], left)
+
+    def send_late(e):
         pltpu.make_async_copy(
-            send.at[:, e, pl.ds(0, CAP), :], xs.at[:, e, pl.ds(0, CAP), own], a2a_sem.at[e, 0]
+            late.at[e, :, pl.ds(0, CAP), :], pan.at[e, y, :, pl.ds(0, CAP), :], late_sem.at[e, 0]
         ).start()
         for g in range(RING):
 
-            def dispatch(k, _):
+            def body(k, _):
                 rows = tile(k, CAP)
                 pltpu.make_async_remote_copy(
-                    src_ref=send.at[:, e, rows, :],
-                    dst_ref=xs.at[:, e, rows, own],
+                    src_ref=late.at[e, :, rows, :],
+                    dst_ref=pan.at[e, y, :, rows, :],
                     send_sem=send_sem.at[0],
-                    recv_sem=a2a_sem.at[e, g],
+                    recv_sem=late_sem.at[e, g],
                     device_id=(peer(k, 1), y),
                     device_id_type=MESH,
                 ).start()
                 return 0
 
-            lax.fori_loop(max(1, g * 8), g * 8 + 8, dispatch, 0)
+            lax.fori_loop(max(1, g * 8), g * 8 + 8, body, 0)
+
+    def tokens_relay():
+        local_wait(dys.at[left], dy_sem.at[1])
+        lower = pl.ds(0, TOK // 2)
+        tokens_copy(dys.at[left, lower, :], left, lower, dy_sem.at[3], right)
+        local_wait(dys.at[right], dy_sem.at[2])
+        upper = pl.ds(TOK // 2, TOK // 2)
+        tokens_copy(dys.at[right, upper, :], right, upper, dy_sem.at[4], left)
+
+    def route_early():
+        local_wait(dys.at[y], dy_sem.at[0])
+        local_wait(dys.at[across, pl.ds(0, TOK // 2), :], dy_sem.at[3])
+        local_wait(dys.at[across, pl.ds(TOK // 2, TOK // 2), :], dy_sem.at[4])
+
+        def body(q, _):
+            rows = dot(gated[...], dys[q], ((1,), (0,)))
+            for e in range(LOCAL):
+                early[e, q] = rows[e * ROWS : (e + 1) * ROWS].astype(BF16)
+            return 0
+
+        lax.fori_loop(0, RING, body, 0)
+
+    def send_early(e):
+        pltpu.make_async_copy(
+            early.at[e, :, pl.ds(0, CAP), :], sf.at[e, :, pl.ds(0, CAP), :], early_sem.at[e]
+        ).start()
+
+        def body(k, _):
+            rows = tile(k, CAP)
+            pltpu.make_async_remote_copy(
+                src_ref=early.at[e, :, rows, :],
+                dst_ref=sf.at[e, :, rows, :],
+                send_sem=send_sem.at[11],
+                recv_sem=early_sem.at[e],
+                device_id=(peer(k, 1), y),
+                device_id_type=MESH,
+            ).start()
+            return 0
+
+        lax.fori_loop(1, GROUPS, body, 0)
 
     def share(e, g):
         rows = pl.ds(g * PART, PART)
-        local_wait(xs.at[:, e, rows, own], a2a_sem.at[e, g])
+        local_wait(pan.at[e, y, :, rows, :], late_sem.at[e, g])
         for other, arrive, s in ((right, left_sem, 1), (left, right_sem, 2)):
             pltpu.make_async_remote_copy(
-                src_ref=xs.at[:, e, rows, own],
-                dst_ref=xs.at[:, e, rows, own],
+                src_ref=pan.at[e, y, :, rows, :],
+                dst_ref=pan.at[e, y, :, rows, :],
                 send_sem=send_sem.at[s],
                 recv_sem=arrive.at[e, g],
                 device_id=(me, other),
@@ -140,15 +202,15 @@
 
     def forward(e, g):
         rows = pl.ds(g * PART, PART)
-        for origin, arrived, arrive, other, array, s in (
-            (left, left_sem, lf_sem, right, 0, 3),
-            (right, right_sem, rf_sem, left, 1, 4),
+        cut = 2 - g % 2
+        for origin, arrived, arrive, other, panels, s in (
+            (left, left_sem, lf_sem, right, pl.ds(0, cut), 3),
+            (right, right_sem, rf_sem, left, pl.ds(cut, 3 - cut), 4),
         ):
-            cols = columns(origin)
-            local_wait(xs.at[:, e, rows, cols], arrived.at[e, g])
+            local_wait(pan.at[e, origin, :, rows, :], arrived.at[e, g])
             pltpu.make_async_remote_copy(
-                src_ref=xs.at[array, e, rows, cols],
-                dst_ref=xs.at[array, e, rows, cols],
+                src_ref=pan.at[e, origin, panels, rows, :],
+                dst_ref=pan.at[e, origin, panels, rows, :],
                 send_sem=send_sem.at[s],
                 recv_sem=arrive.at[e, g],
                 device_id=(me, other),
@@ -156,18 +218,25 @@
             ).start()
 
     def arrive_all(e):
-        cols = columns(across)
         for g in range(RING):
             rows = pl.ds(g * PART, PART)
-            local_wait(xs.at[0, e, rows, cols], lf_sem.at[e, g])
-            local_wait(xs.at[1, e, rows, cols], rf_sem.at[e, g])
+            cut = 2 - g % 2
+            local_wait(pan.at[e, across, pl.ds(0, cut), rows, :], lf_sem.at[e, g])
+            local_wait(pan.at[e, across, pl.ds(cut, 3 - cut), rows, :], rf_sem.at[e, g])
+        local_wait(sf.at[e], early_sem.at[e])
+
+    def inputs(e):
+        return jnp.concatenate([pan[e, q, i] for q in range(RING) for i in range(2)], axis=1)
+
+    def scaled(e):
+        return jnp.concatenate([part for q in range(RING) for part in (sf[e, q], pan[e, q, 2])], axis=1)
 
     def hidden_tiles(e, start, stop):
         def body(j, _):
             cols = tile(j, STEP)
-            pre_g[...] = dot(xs[0, e], wg[e, :, cols], ((1,), (0,)))
-            pre_u[...] = dot(xs[0, e], wu[e, :, cols], ((1,), (0,)))
-            pre_h[...] = dot(xs[1, e], wd[e, cols, :], ((1,), (1,)))
+            pre_g[...] = dot(inputs(e), wg[e, :, cols], ((1,), (0,)))
+            pre_u[...] = dot(inputs(e), wu[e, :, cols], ((1,), (0,)))
+            pre_h[...] = dot(scaled(e), wd[e, cols, :], ((1,), (1,)))
 
             def rows_body(i, _):
                 rows = tile(i, 64)
@@ -237,23 +306,18 @@
         lax.fori_loop(1, GROUPS, body, 0)
 
     def weight_tiles(e, which, start, stop):
-        rows_of, others, result, number = (
-            (xs.at[0, e], dgate.at[e], gw_ref, 0),
-            (xs.at[0, e], dup.at[e], uw_ref, 1),
-            (hid.at[e], xs.at[1, e], dw_ref, 2),
-        )[which]
+        others, result = ((dgate, gw_ref), (dup, uw_ref), (None, dw_ref))[which]
 
         def body(j, _):
             cols = tile(j, STEP)
-            grad[number, cols, :] = dot(rows_of[:, cols], others[...], ((0,), (0,))).astype(BF16)
-            pltpu.make_async_copy(grad.at[number, cols, :], result.at[e, cols, :], out_sem.at[e, which]).start()
+            if which == 2:
+                result[e, cols, :] = dot(hid[e, :, cols], scaled(e), ((0,), (0,))).astype(BF16)
+            else:
+                rows_of = jnp.concatenate([pan[e, j, 0], pan[e, j, 1]], axis=1)
+                result[e, cols, :] = dot(rows_of, others[e], ((0,), (0,))).astype(BF16)
             return 0
 
         lax.fori_loop(start, stop, body, 0)
-
-    def weights_wait(e):
-        for which, result in enumerate((gw_ref, uw_ref, dw_ref)):
-            local_wait(result.at[e], out_sem.at[e, which])
 
     def gates_back():
         lanes = lax.broadcasted_iota(jnp.int32, (ROWS, 128), 1)
@@ -295,17 +359,23 @@
         for i in range(3):
             local_wait(gr.at[i], gr_sem.at[i])
         total = gl[0:2, :] + gr[0, 0:2, :] + gr[1, 0:2, :] + gr[2, 0:2, :]
-        gg_ref[...] = total / gates_ref[...]
+        gg_ref[...] = total / gate_rows
 
     gp[...] = jnp.zeros_like(gp)
     gl[...] = jnp.zeros_like(gl)
 
+    send_late(0)
+    tokens_relay()
     for g in range(RING):
         share(0, g)
+    send_late(1)
+    route_early()
+    send_early(0)
     for g in range(RING):
         forward(0, g)
     for g in range(RING):
         share(1, g)
+    send_early(1)
     arrive_all(0)
     for copy in loads[:3]:
         copy.wait()
@@ -325,7 +395,6 @@
     arrive_all(1)
     for copy in loads[3:]:
         copy.wait()
-    weights_wait(0)
     hidden_tiles(1, 0, 4)
     gates_back()
     reduce_first(1)
@@ -345,12 +414,13 @@
         dot(both[:ROWS], back[0], ((0,), (0,))) + dot(both[ROWS:], back[1], ((0,), (0,)))
     ).astype(BF16)
 
-    weights_wait(1)
-    local_wait(send.at[:, :, pl.ds(CAP, ROWS - CAP), :], send_sem.at[0])
+    local_wait(late.at[:, :, pl.ds(CAP, ROWS - CAP), :], send_sem.at[0])
     for s in (1, 2):
-        local_wait(xs.at[:, :, :, own], send_sem.at[s])
+        local_wait(pan.at[:, y], send_sem.at[s])
     for s in (3, 4):
-        local_wait(xs.at[0, :, :, own], send_sem.at[s])
+        local_wait(pan.at[:, y, :, pl.ds(0, ROWS // 2), :], send_sem.at[s])
+    local_wait(dys.at[pl.ds(0, 3)], send_sem.at[10])
+    local_wait(early.at[:, :, pl.ds(CAP, ROWS - CAP), :], send_sem.at[11])
     local_wait(pa, send_sem.at[5])
     local_wait(pb, send_sem.at[6])
     local_wait(ret.at[:, pl.ds(CAP, ROWS - CAP), :], send_sem.at[7])
@@ -358,30 +428,50 @@
     local_wait(gr, send_sem.at[9])
 
 
+def finish(*refs):
+    count = len(refs) // 2
+    sems = refs[-1]
+    copies = []
+    for i in range(count):
+        for part in range(2 if i >= 2 else 1):
+            src, dst = refs[i], refs[count + i]
+            if i >= 2:
+                src, dst = src.at[part], dst.at[part]
+            copies.append(pltpu.make_async_copy(src, dst, sems.at[i, part]))
+    for copy in copies:
+        copy.start()
+    for copy in copies:
+        copy.wait()
+
+
 def on_device(tokens, grad_out, gates, expert_ids, w_gate, w_up, w_down):
     vmem = pl.BlockSpec(memory_space=pltpu.VMEM)
     hbm = pl.BlockSpec(memory_space=pl.ANY)
-    weight = jax.ShapeDtypeStruct((LOCAL, D, F), BF16)
+    weight = pltpu.VMEM((LOCAL, D, F), BF16)
     dma = pltpu.SemaphoreType.DMA
-    grad_tokens, grad_gates, grad_gate, grad_up, grad_down = pl.pallas_call(
+    held = pl.pallas_call(
         kernel,
         name="expert_layer",
         out_shape=(
-            jax.ShapeDtypeStruct((TOK, Q), BF16),
-            jax.ShapeDtypeStruct((2, TOK), F32),
+            pltpu.VMEM((TOK, Q), BF16),
+            pltpu.VMEM((2, TOK), F32),
             weight,
             weight,
             weight,
         ),
         in_specs=[vmem, vmem, vmem, vmem, hbm, hbm, hbm],
-        out_specs=(vmem, vmem, hbm, hbm, hbm),
+        out_specs=(vmem, vmem, vmem, vmem, vmem),
         scratch_shapes=[
             pltpu.VMEM((LOCAL, D, F), BF16),
             pltpu.VMEM((LOCAL, D, F), BF16),
             pltpu.VMEM((LOCAL, F, D), BF16),
             pltpu.VMEM((2, LOCAL * ROWS, TOK), BF16),
-            pltpu.VMEM((2, LOCAL, ROWS, Q), BF16),
-            pltpu.VMEM((2, LOCAL, ROWS, D), BF16),
+            pltpu.VMEM((LOCAL * ROWS, TOK), BF16),
+            pltpu.VMEM((LOCAL, 3, ROWS, LANES), BF16),
+            pltpu.VMEM((LOCAL, RING, ROWS, LANES), BF16),
+            pltpu.VMEM((RING, TOK, LANES), BF16),
+            pltpu.VMEM((LOCAL, RING, 3, ROWS, LANES), BF16),
+            pltpu.VMEM((LOCAL, RING, ROWS, LANES), BF16),
             pltpu.VMEM((ROWS, STEP), F32),
             pltpu.VMEM((ROWS, STEP), F32),
             pltpu.VMEM((ROWS, STEP), F32),
@@ -400,10 +490,11 @@
             pltpu.VMEM((ROWS, 128), BF16),
             pltpu.VMEM((8, TOK), F32),
             pltpu.VMEM((3, 8, TOK), F32),
-            pltpu.VMEM((3, D, F), BF16),
             dma((LOCAL, 3)),
-            dma((10,)),
+            dma((12,)),
             dma((LOCAL, RING)),
+            dma((LOCAL,)),
+            dma((5,)),
             dma((LOCAL, RING)),
             dma((LOCAL, RING)),
             dma((LOCAL, RING)),
@@ -413,12 +504,20 @@
             dma((LOCAL,)),
             dma,
             dma((3,)),
-            dma((LOCAL, 3)),
         ],
         compiler_params=pltpu.CompilerParams(
-            collective_id=0, has_side_effects=True, vmem_limit_bytes=60 * 1024 * 1024
+            collective_id=0, has_side_effects=True, vmem_limit_bytes=48 * 1024 * 1024
         ),
-    )(expert_ids.T, gates.T.astype(F32), tokens, grad_out, w_gate, w_up, w_down)
+    )(expert_ids.T, gates.T, tokens, grad_out, w_gate, w_up, w_down)
+    grad_tokens, grad_gates, grad_gate, grad_up, grad_down = pl.pallas_call(
+        finish,
+        name="finish",
+        out_shape=[jax.ShapeDtypeStruct(a.shape, a.dtype) for a in held],
+        in_specs=[hbm] * 5,
+        out_specs=[hbm] * 5,
+        scratch_shapes=[dma((5, 2))],
+        compiler_params=pltpu.CompilerParams(vmem_limit_bytes=1024 * 1024),
+    )(*held)
     return grad_tokens, grad_gates.T, grad_gate, grad_up, grad_down
 
 

time: 108 us -> 89.1 us (0.82)
  local copies, waits for them, and re-layouts: 13.3 us -> 0 us
  Pallas kernels: 93 us -> 88.4 us
  other arithmetic: 1.26 us -> 0 us
    unnamed x9 -> x0, local copies, waits for them, and re-layouts: 13.3 us -> none
    pallas_call x1 -> x2, Pallas kernels: 93 us -> 88.4 us  [the longest x1 83.6 us: on_device(): pl.pallas_call(kernel, name='expert_layer', out_shape=(pltpu.VMEM((TOK, Q...]
    convert_element_type x1 -> x0, other arithmetic: 1.26 us -> none  [on_device(): gates.T.astype(F32)]
where the time goes in v2:
time: 89.1 us; the launch traced here: 89 us
  Pallas kernels  88.4 us (99%)
    pallas_call x1, Pallas kernels, on_device(): pl.pallas_call(kernel, name='expert_layer', out_shape=(pltpu.VMEM((TOK, Q...  83.6 us
    pallas_call x1, Pallas kernels, on_device(): pl.pallas_call(finish, name='finish', out_shape=[jax.ShapeDtypeStruct(a.s...  4.73 us

profile of v2, /device:TPU:1, one launch (start us, length us, event | category | flops | bytes accessed | tf_op | source)
XLA Modules:
  0.0 89.0 jit_solution(7967579638160193126)
XLA Ops:
  0.6 83.6 %expert_layer.1 = (bf16[256,256]{1,0:T(8,128)(2,1)S(1)}, f32[2,256]{1,0:T(2,128)S(1)}, bf16[2,1024,1024]{2,1,0:T(8,128)(2,1)S(1)}, bf16[2,1024,1024]{2,1,0:T(8,128)(2,1)S(1)}, bf16[2,1024,1024]{2,1,0:T(8,128)(2,1)S(1)}) custom-call(s32[2,256]{1,0:T(2,128)} %bitcast.3, bf16[2,256]{1,0:T(2,128)(2,1)} %bitcast.4, bf16[256,256]{1,0:T(8,128)(2,1)} %tokens_ref.1, ...), custom_call_target="tpu_custom_call" | custom-call | tf_op jit(solution)/shard_map/expert_layer/pallas_call | solution.py:452
  84.3 4.7 %finish.1 = (bf16[256,256]{1,0:T(8,128)(2,1)}, f32[2,256]{1,0:T(2,128)}, bf16[2,1024,1024]{2,1,0:T(8,128)(2,1)}, bf16[2,1024,1024]{2,1,0:T(8,128)(2,1)}, bf16[2,1024,1024]{2,1,0:T(8,128)(2,1)}) custom-call(bf16[256,256]{1,0:T(8,128)(2,1)S(1)} %get-tuple-element.15.refs_0_, f32[2,256]{1,0:T(2,128)S(1)} %get-tuple-element.16.refs_1_, ...), custom_call_target="tpu_custom_call" | custom-call | tf_op jit(solution)/shard_map/finish/pallas_call | solution.py:512

commit v3 on v2

--- a/solution.py
+++ b/solution.py
@@ -21,6 +21,7 @@
 F = 1024
 LANES = 128
 STEP = 256
+HALF = 256
 PART = 128
 
 
@@ -217,79 +218,85 @@
                 device_id_type=MESH,
             ).start()
 
-    def arrive_all(e):
-        for g in range(RING):
+    def arrive(e, h):
+        for g in (2 * h, 2 * h + 1):
             rows = pl.ds(g * PART, PART)
             cut = 2 - g % 2
             local_wait(pan.at[e, across, pl.ds(0, cut), rows, :], lf_sem.at[e, g])
             local_wait(pan.at[e, across, pl.ds(cut, 3 - cut), rows, :], rf_sem.at[e, g])
-        local_wait(sf.at[e], early_sem.at[e])
-
-    def inputs(e):
-        return jnp.concatenate([pan[e, q, i] for q in range(RING) for i in range(2)], axis=1)
-
-    def scaled(e):
-        return jnp.concatenate([part for q in range(RING) for part in (sf[e, q], pan[e, q, 2])], axis=1)
-
-    def hidden_tiles(e, start, stop):
+        if h == 0:
+            local_wait(sf.at[e], early_sem.at[e])
+
+    def inputs(e, rows):
+        return jnp.concatenate([pan[e, q, i, rows] for q in range(RING) for i in range(2)], axis=1)
+
+    def scaled(e, rows):
+        return jnp.concatenate([part for q in range(RING) for part in (sf[e, q, rows], pan[e, q, 2, rows])], axis=1)
+
+    def hidden_tiles(e, h):
+        chunk = slice(h * HALF, (h + 1) * HALF)
+
         def body(j, _):
             cols = tile(j, STEP)
-            pre_g[...] = dot(inputs(e), wg[e, :, cols], ((1,), (0,)))
-            pre_u[...] = dot(inputs(e), wu[e, :, cols], ((1,), (0,)))
-            pre_h[...] = dot(scaled(e), wd[e, cols, :], ((1,), (1,)))
+            pre_g[...] = dot(inputs(e, chunk), wg[e, :, cols], ((1,), (0,)))
+            pre_u[...] = dot(inputs(e, chunk), wu[e, :, cols], ((1,), (0,)))
+            pre_h[...] = dot(scaled(e, chunk), wd[e, cols, :], ((1,), (1,)))
 
             def rows_body(i, _):
-                rows = tile(i, 64)
-                g, u, dh = pre_g[rows, :], pre_u[rows, :], pre_h[rows, :]
+                near = tile(i, 64)
+                rows = pl.ds(pl.multiple_of(h * HALF + i * 64, 64), 64)
+                g, u, dh = pre_g[near, :], pre_u[near, :], pre_h[near, :]
                 s = jax.nn.sigmoid(g)
                 act = g * s
-                h = (act * u).astype(BF16)
-                hid[e, rows, cols] = h
+                value = (act * u).astype(BF16)
+                hid[e, rows, cols] = value
                 dgate[e, rows, cols] = (dh * u * s * (1.0 + g * (1.0 - s))).astype(BF16)
                 dup[e, rows, cols] = (dh * act).astype(BF16)
-                product = h.astype(F32) * dh
+                product = value.astype(F32) * dh
                 gp[e, rows, :] += product[:, :128] + product[:, 128:]
                 return 0
 
-            lax.fori_loop(0, ROWS // 64, rows_body, 0)
+            lax.fori_loop(0, HALF // 64, rows_body, 0)
             return 0
 
-        lax.fori_loop(start, stop, body, 0)
-
-    def dx_tile(e, q):
+        lax.fori_loop(0, F // STEP, body, 0)
+
+    def dx_tile(e, h, q):
+        chunk = slice(h * HALF, (h + 1) * HALF)
         rows = columns(q)
-        return dot(dgate[e], wg[e, rows, :], ((1,), (1,))) + dot(dup[e], wu[e, rows, :], ((1,), (1,)))
+        return dot(dgate[e, chunk], wg[e, rows, :], ((1,), (1,))) + dot(dup[e, chunk], wu[e, rows, :], ((1,), (1,)))
 
     def ring_copy(src, dst, s, sem, other):
         pltpu.make_async_remote_copy(
             src_ref=src, dst_ref=dst, send_sem=send_sem.at[s], recv_sem=sem, device_id=(me, other), device_id_type=MESH
         ).start()
 
-    half = ROWS // 2
-
-    def reduce_first(e):
-        pa[e] = dx_tile(e, across).astype(BF16)
-        ring_copy(pa.at[e, pl.ds(0, half)], ra.at[e, 0], 5, ra_sem.at[e, 0], right)
-        ring_copy(pa.at[e, pl.ds(half, half)], ra.at[e, 1], 5, ra_sem.at[e, 1], left)
-
-    def reduce_second(e):
-        pre_g[...] = dx_tile(e, right)
-        local_wait(ra.at[e, 0], ra_sem.at[e, 0])
-        pb[e, 0, :half] = (pre_g[:half] + ra[e, 0].astype(F32)).astype(BF16)
-        pb[e, 0, half:] = pre_g[half:].astype(BF16)
-        ring_copy(pb.at[e, 0], rb.at[e, 0], 6, rb_sem.at[e, 0], right)
-        pre_g[...] = dx_tile(e, left)
-        local_wait(ra.at[e, 1], ra_sem.at[e, 1])
-        pb[e, 1, :half] = pre_g[:half].astype(BF16)
-        pb[e, 1, half:] = (pre_g[half:] + ra[e, 1].astype(F32)).astype(BF16)
-        ring_copy(pb.at[e, 1], rb.at[e, 1], 6, rb_sem.at[e, 1], left)
-        red[e] = dx_tile(e, y)
-
-    def give_back(e):
-        local_wait(rb.at[e, 0], rb_sem.at[e, 0])
-        local_wait(rb.at[e, 1], rb_sem.at[e, 1])
-        ret[e] = (red[e] + rb[e, 0].astype(F32) + rb[e, 1].astype(F32)).astype(BF16)
-        pltpu.make_async_copy(ret.at[e, pl.ds(0, CAP), :], back.at[e, pl.ds(0, CAP), :], back_sem.at[e]).start()
+    def reduce_first(e, h):
+        pa[e, h] = dx_tile(e, h, across).astype(BF16)
+        ring_copy(pa.at[e, h, pl.ds(0, PART)], ra.at[e, h, 0], 5, ra_sem.at[e, h, 0], right)
+        ring_copy(pa.at[e, h, pl.ds(PART, PART)], ra.at[e, h, 1], 5, ra_sem.at[e, h, 1], left)
+
+    def reduce_second(e, h):
+        part = dx_tile(e, h, right)
+        local_wait(ra.at[e, h, 0], ra_sem.at[e, h, 0])
+        pb[e, h, 0, :PART] = (part[:PART] + ra[e, h, 0].astype(F32)).astype(BF16)
+        pb[e, h, 0, PART:] = part[PART:].astype(BF16)
+        ring_copy(pb.at[e, h, 0], rb.at[e, h, 0], 6, rb_sem.at[e, h, 0], right)
+        part = dx_tile(e, h, left)
+        local_wait(ra.at[e, h, 1], ra_sem.at[e, h, 1])
+        pb[e, h, 1, :PART] = part[:PART].astype(BF16)
+        pb[e, h, 1, PART:] = (part[PART:] + ra[e, h, 1].astype(F32)).astype(BF16)
+        ring_copy(pb.at[e, h, 1], rb.at[e, h, 1], 6, rb_sem.at[e, h, 1], left)
+        red[e, h] = dx_tile(e, h, y)
+
+    def give_back(e, h):
+        local_wait(rb.at[e, h, 0], rb_sem.at[e, h, 0])
+        local_wait(rb.at[e, h, 1], rb_sem.at[e, h, 1])
+        ret[e, h * HALF : (h + 1) * HALF] = (
+            red[e, h] + rb[e, h, 0].astype(F32) + rb[e, h, 1].astype(F32)
+        ).astype(BF16)
+        if h == 0:
+            pltpu.make_async_copy(ret.at[e, pl.ds(0, CAP), :], back.at[e, pl.ds(0, CAP), :], back_sem.at[e]).start()
 
         def body(k, _):
             rows = tile(k, CAP)
@@ -303,7 +310,7 @@
             ).start()
             return 0
 
-        lax.fori_loop(1, GROUPS, body, 0)
+        lax.fori_loop(1 if h == 0 else GROUPS // 2, GROUPS // 2 * (h + 1), body, 0)
 
     def weight_tiles(e, which, start, stop):
         others, result = ((dgate, gw_ref), (dup, uw_ref), (None, dw_ref))[which]
@@ -311,7 +318,7 @@
         def body(j, _):
             cols = tile(j, STEP)
             if which == 2:
-                result[e, cols, :] = dot(hid[e, :, cols], scaled(e), ((0,), (0,))).astype(BF16)
+                result[e, cols, :] = dot(hid[e, :, cols], scaled(e, slice(0, ROWS)), ((0,), (0,))).astype(BF16)
             else:
                 rows_of = jnp.concatenate([pan[e, j, 0], pan[e, j, 1]], axis=1)
                 result[e, cols, :] = dot(rows_of, others[e], ((0,), (0,))).astype(BF16)
@@ -376,43 +383,52 @@
     for g in range(RING):
         share(1, g)
     send_early(1)
-    arrive_all(0)
+    arrive(0, 0)
     for copy in loads[:3]:
         copy.wait()
-    hidden_tiles(0, 0, 3)
+    hidden_tiles(0, 0)
     forward(1, 0)
-    hidden_tiles(0, 3, 4)
-    reduce_first(0)
+    reduce_first(0, 0)
+    forward(1, 1)
+    arrive(0, 1)
+    hidden_tiles(0, 1)
+    forward(1, 2)
+    reduce_first(0, 1)
     weight_tiles(0, 0, 0, 2)
-    forward(1, 1)
-    reduce_second(0)
-    forward(1, 2)
+    forward(1, 3)
     weight_tiles(0, 0, 2, 4)
-    weight_tiles(0, 1, 0, 4)
-    forward(1, 3)
-    give_back(0)
-    weight_tiles(0, 2, 0, 4)
-    arrive_all(1)
+    weight_tiles(0, 1, 0, 2)
+    arrive(1, 0)
     for copy in loads[3:]:
         copy.wait()
-    hidden_tiles(1, 0, 4)
+    hidden_tiles(1, 0)
+    reduce_first(1, 0)
+    reduce_second(0, 0)
+    reduce_second(0, 1)
+    arrive(1, 1)
+    hidden_tiles(1, 1)
+    reduce_first(1, 1)
     gates_back()
-    reduce_first(1)
+    give_back(0, 0)
+    give_back(0, 1)
+    reduce_second(1, 0)
+    weight_tiles(0, 1, 2, 4)
+    reduce_second(1, 1)
+    weight_tiles(0, 2, 0, 4)
+    give_back(1, 0)
+    gates_share()
     weight_tiles(1, 0, 0, 2)
-    reduce_second(1)
-    gates_share()
+    give_back(1, 1)
     weight_tiles(1, 0, 2, 4)
     weight_tiles(1, 1, 0, 4)
-    give_back(1)
     weight_tiles(1, 2, 0, 4)
     gates_finish()
 
+    both = (route[0].astype(F32) + route[1].astype(F32)).astype(BF16)
     local_wait(back.at[0], back_sem.at[0])
+    first = dot(both[:ROWS], back[0], ((0,), (0,)))
     local_wait(back.at[1], back_sem.at[1])
-    both = (route[0].astype(F32) + route[1].astype(F32)).astype(BF16)
-    out_ref[...] = (
-        dot(both[:ROWS], back[0], ((0,), (0,))) + dot(both[ROWS:], back[1], ((0,), (0,)))
-    ).astype(BF16)
+    out_ref[...] = (first + dot(both[ROWS:], back[1], ((0,), (0,)))).astype(BF16)
 
     local_wait(late.at[:, :, pl.ds(CAP, ROWS - CAP), :], send_sem.at[0])
     for s in (1, 2):
@@ -472,17 +488,17 @@
             pltpu.VMEM((RING, TOK, LANES), BF16),
             pltpu.VMEM((LOCAL, RING, 3, ROWS, LANES), BF16),
             pltpu.VMEM((LOCAL, RING, ROWS, LANES), BF16),
-            pltpu.VMEM((ROWS, STEP), F32),
-            pltpu.VMEM((ROWS, STEP), F32),
-            pltpu.VMEM((ROWS, STEP), F32),
+            pltpu.VMEM((HALF, STEP), F32),
+            pltpu.VMEM((HALF, STEP), F32),
+            pltpu.VMEM((HALF, STEP), F32),
             pltpu.VMEM((LOCAL, ROWS, F), BF16),
             pltpu.VMEM((LOCAL, ROWS, F), BF16),
             pltpu.VMEM((LOCAL, ROWS, F), BF16),
-            pltpu.VMEM((LOCAL, ROWS, Q), BF16),
-            pltpu.VMEM((LOCAL, 2, ROWS, Q), BF16),
-            pltpu.VMEM((LOCAL, 2, ROWS // 2, Q), BF16),
-            pltpu.VMEM((LOCAL, 2, ROWS, Q), BF16),
-            pltpu.VMEM((LOCAL, ROWS, Q), F32),
+            pltpu.VMEM((LOCAL, 2, HALF, Q), BF16),
+            pltpu.VMEM((LOCAL, 2, 2, HALF, Q), BF16),
+            pltpu.VMEM((LOCAL, 2, 2, PART, Q), BF16),
+            pltpu.VMEM((LOCAL, 2, 2, HALF, Q), BF16),
+            pltpu.VMEM((LOCAL, 2, HALF, Q), F32),
             pltpu.VMEM((LOCAL, ROWS, Q), BF16),
             pltpu.VMEM((LOCAL, ROWS, Q), BF16),
             pltpu.VMEM((LOCAL, ROWS, 128), F32),
@@ -499,8 +515,8 @@
             dma((LOCAL, RING)),
             dma((LOCAL, RING)),
             dma((LOCAL, RING)),
-            dma((LOCAL, 2)),
-            dma((LOCAL, 2)),
+            dma((LOCAL, 2, 2)),
+            dma((LOCAL, 2, 2)),
             dma((LOCAL,)),
             dma,
             dma((3,)),

time: 89.1 us -> 77.3 us (0.87)
  Pallas kernels: 88.4 us -> 76.5 us
    pallas_call x1, Pallas kernels: 83.6 us -> 71.8 us  [on_device(): pl.pallas_call(kernel, name='expert_layer', out_shape=(pltpu.VMEM((TOK, Q...]
where the time goes in v3:
time: 77.3 us; the launch traced here: 77.2 us
  Pallas kernels  76.5 us (99%)
    pallas_call x1, Pallas kernels, on_device(): pl.pallas_call(kernel, name='expert_layer', out_shape=(pltpu.VMEM((TOK, Q...  71.8 us
    pallas_call x1, Pallas kernels, on_device(): pl.pallas_call(finish, name='finish', out_shape=[jax.ShapeDtypeStruct(a.s...  4.73 us

profile of v3, /device:TPU:1, one launch (start us, length us, event | category | flops | bytes accessed | tf_op | source)
XLA Modules:
  0.0 77.2 jit_solution(567019140986660056)
XLA Ops:
  0.6 71.8 %expert_layer.1 = (bf16[256,256]{1,0:T(8,128)(2,1)S(1)}, f32[2,256]{1,0:T(2,128)S(1)}, bf16[2,1024,1024]{2,1,0:T(8,128)(2,1)S(1)}, bf16[2,1024,1024]{2,1,0:T(8,128)(2,1)S(1)}, bf16[2,1024,1024]{2,1,0:T(8,128)(2,1)S(1)}) custom-call(s32[2,256]{1,0:T(2,128)} %bitcast.3, bf16[2,256]{1,0:T(2,128)(2,1)} %bitcast.4, bf16[256,256]{1,0:T(8,128)(2,1)} %tokens_ref.1, ...), custom_call_target="tpu_custom_call" | custom-call | tf_op jit(solution)/shard_map/expert_layer/pallas_call | solution.py:468
  72.4 4.7 %finish.1 = (bf16[256,256]{1,0:T(8,128)(2,1)}, f32[2,256]{1,0:T(2,128)}, bf16[2,1024,1024]{2,1,0:T(8,128)(2,1)}, bf16[2,1024,1024]{2,1,0:T(8,128)(2,1)}, bf16[2,1024,1024]{2,1,0:T(8,128)(2,1)}) custom-call(bf16[256,256]{1,0:T(8,128)(2,1)S(1)} %get-tuple-element.15.refs_0_, f32[2,256]{1,0:T(2,128)S(1)} %get-tuple-element.16.refs_1_, ...), custom_call_target="tpu_custom_call" | custom-call | tf_op jit(solution)/shard_map/finish/pallas_call | solution.py:528
